TPU v7x, 32 devices: a whole 2x2x4 slice. The times are simulated.
32 devices in a mesh: facet: 8 (over z, y), col: 4 (over x, core).
Axes of the slice: x: 2, y: 2, z: 4, core: 2. Of those that a mesh axis runs over, the one named last changes fastest.
Arguments:
- prepared: bfloat16 [8, 2, 8192, 512], P('facet', None, None, 'col'), may hold values from -6 to 6
- sub_off: int32 [8, 4], P(None, 'col'), may hold values from 0 to 8191
- fac_off: int32 [8], replicated, may hold values from 0 to 511
- win_col: int32 [4, 128], replicated, may hold values from 0 to 255
- vis_weights: bfloat16 [8, 2, 512, 512], P('facet', None, None, 'col'), may hold values from -6 to 6
Outputs:
- facet_strips: bfloat16 [8, 2, 8192, 256], P('facet', None, 'col')
All inputs are finite; a program needn't handle non-finite values.
Results may differ from a plain program's by a relative error of at most 0.0093.
Values may be sent and summed in bfloat16 or wider, within the bound.
A program may use at most 128 MiB of HBM per device.

v0:
```python
import functools
import math

import jax
import jax.numpy as jnp
import numpy as np
from jax import lax
from jax.experimental import pallas as pl
from jax.experimental.pallas import tpu as pltpu
from jax.sharding import PartitionSpec as P

XM = 128
ALIGN = 16
CHUNKS = 8
OUT_CHUNKS = 8
LAG = 8
MESH = pl.DeviceIdType.MESH
F32 = jnp.float32
BF16 = jnp.bfloat16


def dft(length, sign, scaling):
    ids = np.arange(length)
    angles = 2.0 * np.pi / length * (ids[:, None] * ids[None, :] % length)
    return np.cos(angles) * scaling, sign * np.sin(angles) * scaling


def stacked(real_part, imag_part, axis):
    return np.concatenate([real_part, imag_part], axis=axis).astype(jnp.bfloat16)


def window_tables(length):
    taper = 0.3 + 0.7 * np.sin(np.pi * (np.arange(length) + 0.5) / length) ** 2
    scaling = 1.0 / math.sqrt(length)
    fwd_re, fwd_im = dft(length, -1.0, scaling)
    back_re, back_im = dft(length, 1.0, scaling)
    forward = stacked(fwd_re * taper[None, :], fwd_im * taper[None, :], 0)
    backward = stacked(back_re * taper[:, None], back_im * taper[:, None], 1)
    return forward, backward


def mm(a, b):
    return jnp.dot(a, b, preferred_element_type=F32)


def iota(shape, dim):
    return lax.broadcasted_iota(jnp.int32, shape, dim)


def one_hot(hit):
    return jnp.where(hit, 1.0, 0.0).astype(BF16)


def exchange_kernel(
    nf, ncol, starts, fac, prep, wts, fwd, bwd, win, fmap, qtab,
    terms, starts_all, maps_out,
    pv, qv, wv, send1, recv1, acc, grid, send2, ctab, maps, svec, fv, wdup,
    ld, s1, r1, s2, sx, sp, rt, ss, rs,
):
    me = lax.axis_index("facet")
    c = lax.axis_index("col")
    nx = ncol // 2
    xq, core = lax.div(c, 2), lax.rem(c, 2)
    partner = xq * 2 + 1 - core
    pow2 = nf & (nf - 1) == 0
    blocks = prep.shape[1]
    xa, width = wts.shape[1:]
    half = width // 2
    oc = fmap.shape[0]
    chunks = CHUNKS
    deep = nf <= 8
    step = blocks // chunks

    def peer(i):
        if not pow2:
            return lax.rem(me + i, nf)
        out, b = 0, 1
        while b < nf:
            mb, ib = lax.rem(lax.div(me, b), 2), lax.rem(lax.div(i, b), 2)
            out = out + b * (mb + ib - 2 * mb * ib)
            b *= 2
        return out

    def source(i):
        return peer(i) if pow2 else lax.rem(me + nf - i, nf)

    barrier = pltpu.get_barrier_semaphore()

    @pl.loop(1, nf)
    def _(i):
        pl.semaphore_signal(barrier, inc=1, device_id={"facet": peer(i)}, device_id_type=MESH)

    for i in range(1, ncol):
        pl.semaphore_signal(
            barrier, inc=1, device_id={"col": lax.rem(c + i, ncol)}, device_id_type=MESH
        )

    loads = [
        pltpu.make_async_copy(
            prep.at[:, pl.ds(k * step, step)], pv.at[:, pl.ds(k * step, step)], ld.at[k]
        )
        for k in range(chunks)
    ]
    w_load = pltpu.make_async_copy(wts, wv, ld.at[chunks])
    q_load = pltpu.make_async_copy(qtab, qv, ld.at[chunks + 1])
    f_load = pltpu.make_async_copy(fmap, fv, ld.at[chunks + 2])
    f_load.start()
    for copy in loads:
        copy.start()
    w_load.start()
    q_load.start()

    lane = iota(svec.shape, 1)
    row = jnp.zeros(svec.shape, jnp.int32)
    svec[...] = lax.fori_loop(0, nf, lambda j, v: jnp.where(lane == j, starts[j], v), row)

    def remote(src, dst, send, recv, **where):
        return pltpu.make_async_remote_copy(
            src_ref=src, dst_ref=dst, send_sem=send, recv_sem=recv,
            device_id=where, device_id_type=MESH,
        )

    def send_first(h, j):
        return remote(send1.at[h, j], recv1.at[h, me], s1.at[h, j], r1.at[h, me], facet=j)

    def recv_first(h, j):
        return remote(send1.at[h, j], recv1.at[h, j], s1.at[h, j], r1.at[h, j], facet=j)

    def send_second(h, j):
        return remote(send2.at[h, j], terms.at[c, me, h], s2.at[h, j], rt.at[c, me, h], facet=j)

    def arrival(cc, j, h):
        return remote(send2.at[h, j], terms.at[cc, j, h], s2.at[h, j], rt.at[cc, j, h], facet=j)

    def forward_x(src, j, h, q):
        return remote(
            src, terms.at[c, j, h], sx.at[q, j, h], rt.at[c, j, h],
            col=lax.rem(xq + q, nx) * 2 + core,
        )

    def forward_partner(src, cc, j, h):
        return remote(src, terms.at[cc, j, h], sp.at[cc, j, h], rt.at[cc, j, h], col=partner)

    row_d = iota((XM, 2 * XM), 1) - iota((XM, 2 * XM), 0)
    fwd_table = fwd[...]

    def contribution(j, dst):
        start = starts[j]
        block = lax.div(start, XM)
        shift = lax.rem(start, XM)
        above = lax.rem(block + 1, blocks)
        top = jnp.concatenate([pv[0, block], pv[1, block]], axis=1)
        low = jnp.concatenate([pv[0, above], pv[1, above]], axis=1)
        picked = mm(one_hot(row_d == shift), jnp.concatenate([top, low], axis=0))
        prod = mm(fwd_table, picked.astype(BF16))
        re = prod[:XM, :width] - prod[XM:, width:]
        im = prod[:XM, width:] + prod[XM:, :width]
        first = iota(re.shape, 1) < half
        dst[0, j] = jnp.where(first, re, pltpu.roll(im, half, 1)).astype(BF16)
        dst[1, j] = jnp.where(first, pltpu.roll(re, half, 1), im).astype(BF16)

    def window_maps():
        f_load.wait()
        fm = fv[...]
        col_n = iota((oc, width), 0)
        for k in range(ncol):
            m = lax.dot_general(
                one_hot(col_n == win[k : k + 1, :]), fm, (((0,), (0,)), ((), ())),
                preferred_element_type=F32,
            ).astype(BF16)
            m_re, m_im = m[:, :oc], m[:, oc:]
            upper = jnp.concatenate([m_re, m_im], axis=1)
            lower = jnp.concatenate([-m_im, m_re], axis=1)
            maps[k] = jnp.concatenate(
                [upper[:half], lower[:half], upper[half:], lower[half:]], axis=0
            )

    map_copy = pltpu.make_async_copy(maps, maps_out, ld.at[chunks + 4])
    window_maps()
    map_copy.start()
    for copy in loads:
        copy.wait()
    pl.semaphore_wait(barrier, nf - 1 + ncol - 1)

    @pl.loop(1, nf, unroll=deep)
    def _(i):
        j = peer(nf - i)
        contribution(j, send1)
        send_first(0, j).start()

    @pl.loop(1, nf)
    def _(i):
        send_first(1, peer(nf - i)).start()

    contribution(me, recv1)

    start_sends = []
    for i in range(1, ncol):
        to = lax.rem(c + i, ncol)
        start_sends.append(remote(svec, starts_all.at[c], ss.at[i], rs.at[c], col=to))
        start_sends[-1].start()
    own_starts = pltpu.make_async_copy(svec, starts_all.at[c], ld.at[chunks + 3])
    own_starts.start()

    turn_d = iota((XM, XM), 0) - iota((XM, XM), 1)
    turn_by = lax.rem(starts[me], ALIGN)
    turn = (turn_d == turn_by) | (turn_d == turn_by - XM)
    turned = mm(one_hot(turn), bwd[...]).astype(BF16)
    turned = jnp.concatenate([turned[:, :XM], turned[:, XM:]], axis=0)
    back_d = iota((XM, xa), 1) - iota((XM, xa), 0)

    @pl.loop(0, nf, unroll=deep)
    def _(j):
        hit = (back_d == fac[j]) | (back_d == fac[j] - xa)
        ctab[j] = mm(turned, one_hot(hit)).astype(BF16)

    w_load.wait()
    near = iota((xa, width), 1) < half
    for p in range(2):
        w = wv[p].astype(F32)
        swapped = pltpu.roll(w, half, 1)
        wdup[0, p] = jnp.where(near, w, swapped)
        wdup[1, p] = jnp.where(near, swapped, w)

    grid_d = iota((xa, XM), 0) - iota((xa, XM), 1)

    def place(h, j):
        hit = (grid_d == fac[j]) | (grid_d == fac[j] - xa)
        return mm(one_hot(hit), recv1[h, j])

    def twist(prod, conj):
        n = prod.shape[0] // 2
        crossed = pltpu.roll(prod[n:], half, 1)
        first = iota(crossed.shape, 1) < half
        minus = jnp.logical_not(first) if conj else first
        return prod[:n] + jnp.where(minus, -crossed, crossed)

    own_copies = []
    for h in range(2):
        acc[...] = place(h, me)

        @pl.loop(1, nf)
        def _(i):
            j = source(nf - i)
            recv_first(h, j).wait_recv()
            acc[...] += place(h, j)

        if h == 0:
            q_load.wait()
        table = qv[...]
        spectrum = twist(mm(table, acc[...].astype(BF16)), False)
        crossed = wdup[h, 1] * pltpu.roll(spectrum, half, 1)
        weighted = wdup[h, 0] * spectrum + jnp.where(near, -crossed, crossed)
        image = twist(mm(table, weighted.astype(BF16)), True)
        grid[...] = (image * image_gain(nf, xa)).astype(BF16)

        def back(j):
            return twist(mm(ctab[j], grid[...]), False).astype(BF16)

        send2[h, me] = back(me)
        copy = pltpu.make_async_copy(
            send2.at[h, me], terms.at[c, me, h], ld.at[chunks + 5 + h]
        )
        copy.start()
        own_copies.append(copy)
        for q in range(1, nx):
            forward_x(send2.at[h, me], me, h, q).start()
        forward_partner(send2.at[h, me], c, me, h).start()

        @pl.loop(1, nf, unroll=deep)
        def _(i):
            j = peer(i)
            send2[h, j] = back(j)
            send_second(h, j).start()

    def relay(u):
        h, j = lax.div(u, nf), source(lax.rem(u, nf))
        for q in range(1, nx):
            cc = lax.rem(xq + nx - q, nx) * 2 + core
            arrival(cc, j, h).wait_recv()
            forward_partner(terms.at[cc, j, h], cc, j, h).start()

    @pl.loop(0, 2 * nf)
    def _(u):
        h, i = lax.div(u, nf), lax.rem(u, nf)

        @pl.when(i > 0)
        def _():
            j = source(i)
            arrival(c, j, h).wait_recv()
            for q in range(1, nx):
                forward_x(terms.at[c, j, h], j, h, q).start()
            forward_partner(terms.at[c, j, h], c, j, h).start()

        @pl.when(u >= LAG)
        def _():
            relay(u - LAG)

    @pl.loop(2 * nf - LAG, 2 * nf)
    def _(u):
        relay(u)

    for copy in own_copies:
        copy.wait()
    own_starts.wait()
    map_copy.wait()
    for i in range(1, ncol):
        start_sends[i - 1].wait_send()
        frm = lax.rem(c + ncol - i, ncol)
        remote(svec, starts_all.at[frm], ss.at[i], rs.at[frm], col=frm).wait_recv()

    @pl.loop(0, nf)
    def _(j):
        for h in range(2):
            for q in range(nx):
                cc = lax.rem(xq + q, nx) * 2 + 1 - core
                arrival(cc, j, h).wait_recv()
                mine = lax.rem(xq + q, nx) * 2 + core
                forward_partner(terms.at[c, j, h], mine, j, h).wait_send()
            for q in range(1, nx):
                forward_x(terms.at[c, j, h], j, h, q).wait_send()

    @pl.loop(1, nf)
    def _(i):
        j = peer(i)
        for h in range(2):
            send_first(h, j).wait_send()
            send_second(h, j).wait_send()


def image_gain(nf, xa):
    return math.sqrt(nf * XM) / math.sqrt(xa)


def finish_kernel(nf, ncol, starts_all, terms, maps_in, out, tv, acc, maps, stage, tsem, osem):
    c = lax.axis_index("col")
    own_rows = out.shape[1]
    oc = out.shape[2]
    total = own_rows * ncol
    base = c * own_rows
    count = ncol * nf

    def offset(t):
        cc, j = lax.div(t, nf), lax.rem(t, nf)
        rel = starts_all[cc, 0, j] - base + XM
        rel = jnp.where(rel < 0, rel + total, rel)
        rel = jnp.where(rel >= total, rel - total, rel)
        return cc, j, rel

    def fetch(t, cc, j):
        return pltpu.make_async_copy(terms.at[cc, j], tv.at[t], tsem.at[t])

    map_load = pltpu.make_async_copy(maps_in, maps, tsem.at[count])
    map_load.start()

    @pl.loop(0, count)
    def _(t):
        cc, j, rel = offset(t)

        @pl.when(rel < own_rows + XM)
        def _():
            fetch(t, cc, j).start()

    acc[...] = jnp.zeros_like(acc)
    slot = iota((XM, 2 * oc), 0)
    edge = iota((ALIGN, 2 * oc), 0)
    map_load.wait()

    @pl.loop(0, count)
    def _(t):
        cc, j, rel = offset(t)

        @pl.when(rel < own_rows + XM)
        def _():
            fetch(t, cc, j).wait()
            value = mm(jnp.concatenate([tv[t, 0], tv[t, 1]], axis=1), maps[cc])
            turn = lax.rem(rel, ALIGN)
            low = pl.multiple_of(rel - turn, ALIGN)
            acc[pl.ds(low, XM), :] += jnp.where(slot >= turn, value, 0.0)
            acc[pl.ds(pl.multiple_of(low + XM, ALIGN), ALIGN), :] += jnp.where(
                edge < turn, value[:ALIGN], 0.0
            )

    chunk = own_rows // OUT_CHUNKS
    copies = []
    for k in range(OUT_CHUNKS):
        rows = pl.ds(k * chunk, chunk)
        src = pl.ds(XM + k * chunk, chunk)
        stage[0, rows, :] = acc[src, :oc].astype(BF16)
        stage[1, rows, :] = acc[src, oc:].astype(BF16)
        copy = pltpu.make_async_copy(stage.at[:, rows, :], out.at[:, rows, :], osem.at[k])
        copy.start()
        copies.append(copy)
    for copy in copies:
        copy.wait()


def body(prepared, sub_off, fac_off, win_col, vis_weights):
    nf = fac_off.shape[0]
    ncol = lax.axis_size("col")
    facet_strip = prepared[0]
    facet_len, width = facet_strip.shape[1:]
    strip_blocks = facet_strip.reshape(2, facet_len // XM, XM, width)
    weights = vis_weights[0]
    xa = weights.shape[1]
    oc = width * ncol // 2
    own_rows = facet_len // ncol
    starts = sub_off[:, 0]
    lanes = -(-nf // 128) * 128

    forward, backward = window_tables(XM)
    q_table = stacked(*dft(xa, -1.0, 1.0 / math.sqrt(nf * XM)), 0)
    out_map = stacked(*dft(oc, 1.0, 1.0 / math.sqrt(2 * oc)), 1)

    smem = pl.BlockSpec(memory_space=pltpu.SMEM)
    vmem = pl.BlockSpec(memory_space=pltpu.VMEM)
    hbm = pl.BlockSpec(memory_space=pl.ANY)
    dma = pltpu.SemaphoreType.DMA
    halves = pltpu.VMEM((2, nf, XM, width), BF16)
    maps = (ncol, 2 * width, 2 * oc)
    terms, starts_all, maps_all = pl.pallas_call(
        functools.partial(exchange_kernel, nf, ncol),
        out_shape=(
            jax.ShapeDtypeStruct((ncol, nf, 2, XM, width), BF16),
            jax.ShapeDtypeStruct((ncol, 8, lanes), jnp.int32),
            jax.ShapeDtypeStruct(maps, BF16),
        ),
        in_specs=[smem, smem, hbm, hbm, vmem, vmem, vmem, hbm, hbm],
        out_specs=(hbm, hbm, hbm),
        scratch_shapes=[
            pltpu.VMEM(strip_blocks.shape, BF16),
            pltpu.VMEM(q_table.shape, BF16),
            pltpu.VMEM(weights.shape, BF16),
            halves,
            halves,
            pltpu.VMEM((xa, width), F32),
            pltpu.VMEM((xa, width), BF16),
            halves,
            pltpu.VMEM((nf, 2 * XM, xa), BF16),
            pltpu.VMEM(maps, BF16),
            pltpu.VMEM((8, lanes), jnp.int32),
            pltpu.VMEM(out_map.shape, BF16),
            pltpu.VMEM((2, 2, xa, width), F32),
            dma((CHUNKS + 7,)), dma((2, nf)), dma((2, nf)), dma((2, nf)),
            dma((ncol, nf, 2)), dma((ncol, nf, 2)), dma((ncol, nf, 2)), dma((ncol,)), dma((ncol,)),
        ],
        compiler_params=pltpu.CompilerParams(collective_id=0, has_side_effects=True),
        name="exchange",
    )(
        starts, fac_off, strip_blocks, weights, jnp.asarray(forward), jnp.asarray(backward),
        win_col, jnp.asarray(out_map), jnp.asarray(q_table),
    )
    out = pl.pallas_call(
        functools.partial(finish_kernel, nf, ncol),
        out_shape=jax.ShapeDtypeStruct((2, own_rows, oc), BF16),
        in_specs=[smem, hbm, hbm],
        out_specs=hbm,
        scratch_shapes=[
            pltpu.VMEM((ncol * nf, 2, XM, width), BF16),
            pltpu.VMEM((own_rows + 2 * XM + ALIGN, 2 * oc), F32),
            pltpu.VMEM(maps, BF16),
            pltpu.VMEM((2, own_rows, oc), BF16),
            dma((ncol * nf + 1,)),
            dma((OUT_CHUNKS,)),
        ],
        name="finish",
    )(starts_all, terms, maps_all)
    return out[None]


def solution(mesh):
    in_specs = (
        P("facet", None, None, "col"),
        P(None, "col"),
        P(),
        P(),
        P("facet", None, None, "col"),
    )
    out_specs = P("facet", None, "col", None)
    return jax.shard_map(body, mesh=mesh, in_specs=in_specs, out_specs=out_specs, check_vma=False)
```

profile of v0, /device:TPU:0, one launch (start us, length us, event | category | flops | bytes accessed | tf_op | source)
XLA Modules:
  0.0 47.3 jit_solution(11027079273820577189)
XLA Ops:
  0.0 40.7 %exchange.1 = (bf16[4,8,2,128,128]{4,3,2,1,0:T(8,128)(2,1)}, s32[4,8,128]{2,1,0:T(8,128)}, bf16[4,256,512]{2,1,0:T(8,128)(2,1)}) custom-call(s32[8]{0:T(128)} %bitcast.6, s32[8]{0:T(128)} %fac.1, bf16[2,64,128,128]{3,2,1,0:T(8,128)(2,1)} %bitcast.4, bf16[2,512,128]{2,1,0:T(8,128)(2,1)} %bitcast.5, bf16[256,128]{1,0:T(8,128)(2,1)} %constant.8.clone.fwd, ...), custom_call_target="tpu_custom_call" | custom-call | tf_op jit(solution)/shard_map/exchange/pallas_call | solution.py:421
  40.7 6.6 %finish.1 = bf16[2,2048,256]{2,1,0:T(8,128)(2,1)} custom-call(s32[4,8,128]{2,1,0:T(8,128)} %get-tuple-element.8.starts_all, bf16[4,8,2,128,128]{4,3,2,1,0:T(8,128)(2,1)} %get-tuple-element.9.terms, bf16[4,256,512]{2,1,0:T(8,128)(2,1)} %get-tuple-element.10.maps_in), custom_call_target="tpu_custom_call" | custom-call | tf_op jit(solution)/shard_map/finish/pallas_call | solution.py:453
where the time goes:
time: 47.5 us; the launch traced here: 47.3 us
  Pallas kernels  47.3 us (100%)
    pallas_call x1, Pallas kernels, body(): pl.pallas_call(functools.partial(exchange_kernel, nf, ncol), out_shape=(j...  40.7 us
    pallas_call x1, Pallas kernels, body(): pl.pallas_call(functools.partial(finish_kernel, nf, ncol), out_shape=jax....  6.64 us

commit v1 on v0

--- a/solution.py
+++ b/solution.py
@@ -13,7 +13,8 @@
 ALIGN = 16
 CHUNKS = 8
 OUT_CHUNKS = 8
-LAG = 8
+VALUES_LIMIT = 16 * 2**20
+VMEM_LIMIT = 40 * 2**20
 MESH = pl.DeviceIdType.MESH
 F32 = jnp.float32
 BF16 = jnp.bfloat16
@@ -52,10 +53,10 @@
 
 
 def exchange_kernel(
-    nf, ncol, starts, fac, prep, wts, fwd, bwd, win, fmap, qtab,
-    terms, starts_all, maps_out,
-    pv, qv, wv, send1, recv1, acc, grid, send2, ctab, maps, svec, fv, wdup,
-    ld, s1, r1, s2, sx, sp, rt, ss, rs,
+    nf, ncol, near, early, starts_in, fac_in, prep, wts, fwd_in, bwd_in, win_in, fmap, qtab,
+    terms, values, maps, starts_out,
+    starts, fac, fwd, bwd, win, pv, qv, wv, send1, recv1, acc, grid, send2, ctab, svec, sall, fv, wdup,
+    ld, s1, r1, s2, sd, sx, sp, rt, ss, rs,
 ):
     me = lax.axis_index("facet")
     c = lax.axis_index("col")
@@ -84,6 +85,9 @@
     def source(i):
         return peer(i) if pow2 else lax.rem(me + nf - i, nf)
 
+    def across(q):
+        return lax.rem(xq + q, nx) * 2 + core
+
     barrier = pltpu.get_barrier_semaphore()
 
     @pl.loop(1, nf)
@@ -94,6 +98,13 @@
         pl.semaphore_signal(
             barrier, inc=1, device_id={"col": lax.rem(c + i, ncol)}, device_id_type=MESH
         )
+
+    @pl.loop(1, near)
+    def _(i):
+        for q in range(1, nx):
+            pl.semaphore_signal(
+                barrier, inc=1, device_id={"facet": peer(i), "col": across(q)}, device_id_type=MESH
+            )
 
     loads = [
         pltpu.make_async_copy(
@@ -101,14 +112,15 @@
         )
         for k in range(chunks)
     ]
-    w_load = pltpu.make_async_copy(wts, wv, ld.at[chunks])
-    q_load = pltpu.make_async_copy(qtab, qv, ld.at[chunks + 1])
-    f_load = pltpu.make_async_copy(fmap, fv, ld.at[chunks + 2])
-    f_load.start()
-    for copy in loads:
+    small = [(starts_in, starts), (fac_in, fac), (fwd_in, fwd)]
+    later = [(win_in, win), (fmap, fv), (bwd_in, bwd), (wts, wv), (qtab, qv)]
+    small = [pltpu.make_async_copy(*pair, ld.at[chunks + k]) for k, pair in enumerate(small)]
+    later = [pltpu.make_async_copy(*pair, ld.at[chunks + 3 + k]) for k, pair in enumerate(later)]
+    for copy in small + loads + later:
         copy.start()
-    w_load.start()
-    q_load.start()
+    win_load, f_load, b_load, w_load, q_load = later
+    for copy in small:
+        copy.wait()
 
     lane = iota(svec.shape, 1)
     row = jnp.zeros(svec.shape, jnp.int32)
@@ -129,13 +141,18 @@
     def send_second(h, j):
         return remote(send2.at[h, j], terms.at[c, me, h], s2.at[h, j], rt.at[c, me, h], facet=j)
 
+    def send_direct(h, j, q):
+        return remote(
+            send2.at[h, j], terms.at[c, me, h], sd.at[q, j, h], rt.at[c, me, h],
+            facet=j, col=across(q),
+        )
+
     def arrival(cc, j, h):
         return remote(send2.at[h, j], terms.at[cc, j, h], s2.at[h, j], rt.at[cc, j, h], facet=j)
 
     def forward_x(src, j, h, q):
         return remote(
-            src, terms.at[c, j, h], sx.at[q, j, h], rt.at[c, j, h],
-            col=lax.rem(xq + q, nx) * 2 + core,
+            src, terms.at[c, j, h], sx.at[q, j, h], rt.at[c, j, h], col=across(q)
         )
 
     def forward_partner(src, cc, j, h):
@@ -160,6 +177,7 @@
         dst[1, j] = jnp.where(first, pltpu.roll(re, half, 1), im).astype(BF16)
 
     def window_maps():
+        win_load.wait()
         f_load.wait()
         fm = fv[...]
         col_n = iota((oc, width), 0)
@@ -175,12 +193,9 @@
                 [upper[:half], lower[:half], upper[half:], lower[half:]], axis=0
             )
 
-    map_copy = pltpu.make_async_copy(maps, maps_out, ld.at[chunks + 4])
-    window_maps()
-    map_copy.start()
     for copy in loads:
         copy.wait()
-    pl.semaphore_wait(barrier, nf - 1 + ncol - 1)
+    pl.semaphore_wait(barrier, nf - 1 + ncol - 1 + (near - 1) * (nx - 1))
 
     @pl.loop(1, nf, unroll=deep)
     def _(i):
@@ -197,11 +212,12 @@
     start_sends = []
     for i in range(1, ncol):
         to = lax.rem(c + i, ncol)
-        start_sends.append(remote(svec, starts_all.at[c], ss.at[i], rs.at[c], col=to))
+        start_sends.append(remote(svec, sall.at[c], ss.at[i], rs.at[c], col=to))
         start_sends[-1].start()
-    own_starts = pltpu.make_async_copy(svec, starts_all.at[c], ld.at[chunks + 3])
-    own_starts.start()
-
+    sall[c] = svec[...]
+    window_maps()
+
+    b_load.wait()
     turn_d = iota((XM, XM), 0) - iota((XM, XM), 1)
     turn_by = lax.rem(starts[me], ALIGN)
     turn = (turn_d == turn_by) | (turn_d == turn_by - XM)
@@ -215,12 +231,12 @@
         ctab[j] = mm(turned, one_hot(hit)).astype(BF16)
 
     w_load.wait()
-    near = iota((xa, width), 1) < half
+    near_lane = iota((xa, width), 1) < half
     for p in range(2):
         w = wv[p].astype(F32)
         swapped = pltpu.roll(w, half, 1)
-        wdup[0, p] = jnp.where(near, w, swapped)
-        wdup[1, p] = jnp.where(near, swapped, w)
+        wdup[0, p] = jnp.where(near_lane, w, swapped)
+        wdup[1, p] = jnp.where(near_lane, swapped, w)
 
     grid_d = iota((xa, XM), 0) - iota((xa, XM), 1)
 
@@ -235,6 +251,7 @@
         minus = jnp.logical_not(first) if conj else first
         return prod[:n] + jnp.where(minus, -crossed, crossed)
 
+    q_load.wait()
     own_copies = []
     for h in range(2):
         acc[...] = place(h, me)
@@ -245,12 +262,10 @@
             recv_first(h, j).wait_recv()
             acc[...] += place(h, j)
 
-        if h == 0:
-            q_load.wait()
         table = qv[...]
         spectrum = twist(mm(table, acc[...].astype(BF16)), False)
         crossed = wdup[h, 1] * pltpu.roll(spectrum, half, 1)
-        weighted = wdup[h, 0] * spectrum + jnp.where(near, -crossed, crossed)
+        weighted = wdup[h, 0] * spectrum + jnp.where(near_lane, -crossed, crossed)
         image = twist(mm(table, weighted.astype(BF16)), True)
         grid[...] = (image * image_gain(nf, xa)).astype(BF16)
 
@@ -259,7 +274,7 @@
 
         send2[h, me] = back(me)
         copy = pltpu.make_async_copy(
-            send2.at[h, me], terms.at[c, me, h], ld.at[chunks + 5 + h]
+            send2.at[h, me], terms.at[c, me, h], ld.at[chunks + 8 + h]
         )
         copy.start()
         own_copies.append(copy)
@@ -267,119 +282,161 @@
             forward_x(send2.at[h, me], me, h, q).start()
         forward_partner(send2.at[h, me], c, me, h).start()
 
-        @pl.loop(1, nf, unroll=deep)
+        @pl.loop(1, near, unroll=deep)
         def _(i):
             j = peer(i)
             send2[h, j] = back(j)
             send_second(h, j).start()
-
-    def relay(u):
-        h, j = lax.div(u, nf), source(lax.rem(u, nf))
-        for q in range(1, nx):
-            cc = lax.rem(xq + nx - q, nx) * 2 + core
-            arrival(cc, j, h).wait_recv()
-            forward_partner(terms.at[cc, j, h], cc, j, h).start()
-
-    @pl.loop(0, 2 * nf)
-    def _(u):
-        h, i = lax.div(u, nf), lax.rem(u, nf)
-
-        @pl.when(i > 0)
-        def _():
-            j = source(i)
-            arrival(c, j, h).wait_recv()
             for q in range(1, nx):
-                forward_x(terms.at[c, j, h], j, h, q).start()
-            forward_partner(terms.at[c, j, h], c, j, h).start()
-
-        @pl.when(u >= LAG)
-        def _():
-            relay(u - LAG)
-
-    @pl.loop(2 * nf - LAG, 2 * nf)
-    def _(u):
-        relay(u)
+                send_direct(h, j, q).start()
+
+        @pl.loop(near, nf, unroll=deep)
+        def _(i):
+            j = peer(i)
+            send2[h, j] = back(j)
+            send_second(h, j).start()
 
     for copy in own_copies:
         copy.wait()
-    own_starts.wait()
-    map_copy.wait()
     for i in range(1, ncol):
         start_sends[i - 1].wait_send()
         frm = lax.rem(c + ncol - i, ncol)
-        remote(svec, starts_all.at[frm], ss.at[i], rs.at[frm], col=frm).wait_recv()
-
-    @pl.loop(0, nf)
-    def _(j):
-        for h in range(2):
+        remote(svec, sall.at[frm], ss.at[i], rs.at[frm], col=frm).wait_recv()
+    starts_copy = pltpu.make_async_copy(sall, starts_out, ld.at[chunks + 10])
+    starts_copy.start()
+
+    def relay_near(h):
+        @pl.loop(1, near)
+        def _(i):
+            j = source(i)
+            arrival(c, j, h).wait_recv()
+            forward_partner(terms.at[c, j, h], c, j, h).start()
+
+        @pl.loop(0, near)
+        def _(i):
+            relay_across(source(i), h)
+
+    def relay_far(j, h):
+        arrival(c, j, h).wait_recv()
+        for q in range(1, nx):
+            forward_x(terms.at[c, j, h], j, h, q).start()
+        forward_partner(terms.at[c, j, h], c, j, h).start()
+
+    def relay_across(j, h):
+        for q in range(1, nx):
+            cc = across(q)
+            arrival(cc, j, h).wait_recv()
+            forward_partner(terms.at[cc, j, h], cc, j, h).start()
+
+    def from_partner(j, h):
+        for q in range(nx):
+            arrival(lax.rem(xq + q, nx) * 2 + 1 - core, j, h).wait_recv()
+
+    @pl.loop(near, nf)
+    def _(i):
+        relay_far(source(i), 0)
+
+    relay_near(0)
+    relay_near(1)
+
+    @pl.loop(near, nf)
+    def _(i):
+        relay_far(source(i), 1)
+        relay_across(source(i), 0)
+
+    @pl.loop(0, near)
+    def _(i):
+        j = source(i)
+        from_partner(j, 0)
+        from_partner(j, 1)
+        if early:
+            for k in range(ncol):
+                values[k, i] = mm(jnp.concatenate([terms[k, j, 0], terms[k, j, 1]], axis=1), maps[k])
+
+    @pl.loop(near, nf)
+    def _(i):
+        relay_across(source(i), 1)
+
+    @pl.loop(near, nf)
+    def _(i):
+        from_partner(source(i), 0)
+        from_partner(source(i), 1)
+
+    starts_copy.wait()
+    for h in range(2):
+        @pl.loop(0, nf)
+        def _(j):
             for q in range(nx):
-                cc = lax.rem(xq + q, nx) * 2 + 1 - core
-                arrival(cc, j, h).wait_recv()
-                mine = lax.rem(xq + q, nx) * 2 + core
-                forward_partner(terms.at[c, j, h], mine, j, h).wait_send()
+                forward_partner(terms.at[c, j, h], across(q), j, h).wait_send()
+
+        for q in range(1, nx):
+            forward_x(send2.at[h, me], me, h, q).wait_send()
+
+        @pl.loop(near, nf)
+        def _(i):
+            j = source(i)
             for q in range(1, nx):
                 forward_x(terms.at[c, j, h], j, h, q).wait_send()
 
-    @pl.loop(1, nf)
-    def _(i):
-        j = peer(i)
-        for h in range(2):
-            send_first(h, j).wait_send()
-            send_second(h, j).wait_send()
+        @pl.loop(1, near)
+        def _(i):
+            for q in range(1, nx):
+                send_direct(h, peer(i), q).wait_send()
+
+        @pl.loop(1, nf)
+        def _(i):
+            send_first(h, peer(i)).wait_send()
+            send_second(h, peer(i)).wait_send()
 
 
 def image_gain(nf, xa):
     return math.sqrt(nf * XM) / math.sqrt(xa)
 
 
-def finish_kernel(nf, ncol, starts_all, terms, maps_in, out, tv, acc, maps, stage, tsem, osem):
+def finish_kernel(nf, ncol, near, early, starts_all, terms, values, maps, out, acc, stage, osem):
+    me = lax.axis_index("facet")
     c = lax.axis_index("col")
     own_rows = out.shape[1]
     oc = out.shape[2]
     total = own_rows * ncol
     base = c * own_rows
-    count = ncol * nf
-
-    def offset(t):
-        cc, j = lax.div(t, nf), lax.rem(t, nf)
-        rel = starts_all[cc, 0, j] - base + XM
-        rel = jnp.where(rel < 0, rel + total, rel)
-        rel = jnp.where(rel >= total, rel - total, rel)
-        return cc, j, rel
-
-    def fetch(t, cc, j):
-        return pltpu.make_async_copy(terms.at[cc, j], tv.at[t], tsem.at[t])
-
-    map_load = pltpu.make_async_copy(maps_in, maps, tsem.at[count])
-    map_load.start()
-
-    @pl.loop(0, count)
-    def _(t):
-        cc, j, rel = offset(t)
-
-        @pl.when(rel < own_rows + XM)
-        def _():
-            fetch(t, cc, j).start()
+    pow2 = nf & (nf - 1) == 0
+
+    def source(i):
+        if not pow2:
+            return lax.rem(me + nf - i, nf)
+        return jnp.bitwise_xor(me, i)
 
     acc[...] = jnp.zeros_like(acc)
     slot = iota((XM, 2 * oc), 0)
     edge = iota((ALIGN, 2 * oc), 0)
-    map_load.wait()
-
-    @pl.loop(0, count)
-    def _(t):
-        cc, j, rel = offset(t)
-
-        @pl.when(rel < own_rows + XM)
-        def _():
-            fetch(t, cc, j).wait()
-            value = mm(jnp.concatenate([tv[t, 0], tv[t, 1]], axis=1), maps[cc])
-            turn = lax.rem(rel, ALIGN)
-            low = pl.multiple_of(rel - turn, ALIGN)
-            acc[pl.ds(low, XM), :] += jnp.where(slot >= turn, value, 0.0)
-            acc[pl.ds(pl.multiple_of(low + XM, ALIGN), ALIGN), :] += jnp.where(
-                edge < turn, value[:ALIGN], 0.0
-            )
+
+    def gather(first, last, value_of):
+        @pl.loop(first * ncol, last * ncol)
+        def _(t):
+            i, cc = lax.div(t, ncol), lax.rem(t, ncol)
+            j = source(i)
+            rel = starts_all[cc, 0, j] - base + XM
+            rel = jnp.where(rel < 0, rel + total, rel)
+            rel = jnp.where(rel >= total, rel - total, rel)
+
+            @pl.when(rel < own_rows + XM)
+            def _():
+                value = value_of(cc, i, j)
+                turn = lax.rem(rel, ALIGN)
+                low = pl.multiple_of(rel - turn, ALIGN)
+                acc[pl.ds(low, XM), :] += jnp.where(slot >= turn, value, 0.0)
+                acc[pl.ds(pl.multiple_of(low + XM, ALIGN), ALIGN), :] += jnp.where(
+                    edge < turn, value[:ALIGN], 0.0
+                )
+
+    def mapped(cc, i, j):
+        return mm(jnp.concatenate([terms[cc, j, 0], terms[cc, j, 1]], axis=1), maps[cc])
+
+    split = near if early else 0
+    if early:
+        gather(0, split, lambda cc, i, j: values[cc, i])
+    gather(split, nf, mapped)
 
     chunk = own_rows // OUT_CHUNKS
     copies = []
@@ -407,6 +464,8 @@
     own_rows = facet_len // ncol
     starts = sub_off[:, 0]
     lanes = -(-nf // 128) * 128
+    near = nf // 2 if nf & (nf - 1) == 0 else 1
+    early = ncol * near * XM * 2 * oc * 4 <= VALUES_LIMIT
 
     forward, backward = window_tables(XM)
     q_table = stacked(*dft(xa, -1.0, 1.0 / math.sqrt(nf * XM)), 0)
@@ -417,17 +476,27 @@
     hbm = pl.BlockSpec(memory_space=pl.ANY)
     dma = pltpu.SemaphoreType.DMA
     halves = pltpu.VMEM((2, nf, XM, width), BF16)
-    maps = (ncol, 2 * width, 2 * oc)
-    terms, starts_all, maps_all = pl.pallas_call(
-        functools.partial(exchange_kernel, nf, ncol),
+    operands = (
+        starts, fac_off, strip_blocks, weights, jnp.asarray(forward), jnp.asarray(backward),
+        win_col, jnp.asarray(out_map), jnp.asarray(q_table),
+    )
+    held = (ncol, near, XM, 2 * oc) if early else (8, 128)
+    results = pl.pallas_call(
+        functools.partial(exchange_kernel, nf, ncol, near, early),
         out_shape=(
-            jax.ShapeDtypeStruct((ncol, nf, 2, XM, width), BF16),
-            jax.ShapeDtypeStruct((ncol, 8, lanes), jnp.int32),
-            jax.ShapeDtypeStruct(maps, BF16),
+            pltpu.VMEM((ncol, nf, 2, XM, width), BF16),
+            pltpu.VMEM(held, F32),
+            pltpu.VMEM((ncol, 2 * width, 2 * oc), BF16),
+            pltpu.SMEM((ncol, 8, lanes), jnp.int32),
         ),
-        in_specs=[smem, smem, hbm, hbm, vmem, vmem, vmem, hbm, hbm],
-        out_specs=(hbm, hbm, hbm),
+        in_specs=[hbm] * len(operands),
+        out_specs=(vmem, vmem, vmem, smem),
         scratch_shapes=[
+            pltpu.SMEM((nf,), jnp.int32),
+            pltpu.SMEM((nf,), jnp.int32),
+            pltpu.VMEM(forward.shape, BF16),
+            pltpu.VMEM(backward.shape, BF16),
+            pltpu.VMEM(win_col.shape, jnp.int32),
             pltpu.VMEM(strip_blocks.shape, BF16),
             pltpu.VMEM(q_table.shape, BF16),
             pltpu.VMEM(weights.shape, BF16),
@@ -437,34 +506,34 @@
             pltpu.VMEM((xa, width), BF16),
             halves,
             pltpu.VMEM((nf, 2 * XM, xa), BF16),
-            pltpu.VMEM(maps, BF16),
             pltpu.VMEM((8, lanes), jnp.int32),
+            pltpu.VMEM((ncol, 8, lanes), jnp.int32),
             pltpu.VMEM(out_map.shape, BF16),
             pltpu.VMEM((2, 2, xa, width), F32),
-            dma((CHUNKS + 7,)), dma((2, nf)), dma((2, nf)), dma((2, nf)),
-            dma((ncol, nf, 2)), dma((ncol, nf, 2)), dma((ncol, nf, 2)), dma((ncol,)), dma((ncol,)),
+            dma((CHUNKS + 11,)), dma((2, nf)), dma((2, nf)), dma((2, nf)),
+            dma((ncol, nf, 2)), dma((ncol, nf, 2)), dma((ncol, nf, 2)), dma((ncol, nf, 2)),
+            dma((ncol,)), dma((ncol,)),
         ],
-        compiler_params=pltpu.CompilerParams(collective_id=0, has_side_effects=True),
+        compiler_params=pltpu.CompilerParams(
+            collective_id=0, has_side_effects=True, vmem_limit_bytes=VMEM_LIMIT
+        ),
         name="exchange",
-    )(
-        starts, fac_off, strip_blocks, weights, jnp.asarray(forward), jnp.asarray(backward),
-        win_col, jnp.asarray(out_map), jnp.asarray(q_table),
-    )
+    )(*[pltpu.with_memory_space_constraint(x, pltpu.HBM) for x in operands])
+    terms, values, maps, starts_all = results
+    spaces = (pltpu.SMEM, pltpu.VMEM, pltpu.VMEM, pltpu.VMEM)
     out = pl.pallas_call(
-        functools.partial(finish_kernel, nf, ncol),
+        functools.partial(finish_kernel, nf, ncol, near, early),
         out_shape=jax.ShapeDtypeStruct((2, own_rows, oc), BF16),
-        in_specs=[smem, hbm, hbm],
+        in_specs=[smem, vmem, vmem, vmem],
         out_specs=hbm,
         scratch_shapes=[
-            pltpu.VMEM((ncol * nf, 2, XM, width), BF16),
             pltpu.VMEM((own_rows + 2 * XM + ALIGN, 2 * oc), F32),
-            pltpu.VMEM(maps, BF16),
             pltpu.VMEM((2, own_rows, oc), BF16),
-            dma((ncol * nf + 1,)),
             dma((OUT_CHUNKS,)),
         ],
+        compiler_params=pltpu.CompilerParams(vmem_limit_bytes=VMEM_LIMIT),
         name="finish",
-    )(starts_all, terms, maps_all)
+    )(*[pltpu.with_memory_space_constraint(x, m) for x, m in zip((starts_all, terms, values, maps), spaces)])
     return out[None]
 
 

time: 47.5 us -> 43.8 us (0.922)
  Pallas kernels: 47.3 us -> 43.8 us
    pallas_call x2, Pallas kernels: 47.3 us -> 43.8 us  [the longest x1 39.7 us: body(): pl.pallas_call(functools.partial(exchange_kernel, nf, ncol, near, early),...]
where the time goes in v1:
time: 43.8 us
  Pallas kernels  43.8 us (100%)
    pallas_call x1, Pallas kernels, body(): pl.pallas_call(functools.partial(exchange_kernel, nf, ncol, near, early),...  39.7 us
    pallas_call x1, Pallas kernels, body(): pl.pallas_call(functools.partial(finish_kernel, nf, ncol, near, early), o...  4.06 us

profile of v1, /device:TPU:0, one launch (start us, length us, event | category | flops | bytes accessed | tf_op | source)
XLA Modules:
  0.0 43.8 jit_solution(6070054910694651995)
XLA Ops:
  0.0 39.7 %exchange.1 = (bf16[4,8,2,128,128]{4,3,2,1,0:T(8,128)(2,1)S(1)}, f32[4,4,128,512]{3,2,1,0:T(8,128)S(1)}, bf16[4,256,512]{2,1,0:T(8,128)(2,1)S(1)}, s32[4,8,128]{2,1,0:T(8,128)S(4)}) custom-call(s32[8]{0:T(128)} %bitcast.6, s32[8]{0:T(128)} %fac_in.1, bf16[2,64,128,128]{3,2,1,0:T(8,128)(2,1)} %bitcast.4, bf16[2,512,128]{2,1,0:T(8,128)(2,1)} %bitcast.5, ...), custom_call_target="tpu_custom_call" | custom-call | tf_op jit(solution)/shard_map/exchange/pallas_call | solution.py:484
  39.7 4.1 %finish.1 = bf16[2,2048,256]{2,1,0:T(8,128)(2,1)} custom-call(s32[4,8,128]{2,1,0:T(8,128)S(4)} %get-tuple-element.9.starts_all, bf16[4,8,2,128,128]{4,3,2,1,0:T(8,128)(2,1)S(1)} %get-tuple-element.10.terms, f32[4,4,128,512]{3,2,1,0:T(8,128)S(1)} %get-tuple-element.11.values, bf16[4,256,512]{2,1,0:T(8,128)(2,1)S(1)} %get-tuple-element.12.maps), custom_call_target="tpu_custom_call" | custom-call | tf_op jit(solution)/shard_map/finish/pallas_call | solution.py:524

commit v2 on v1

--- a/solution.py
+++ b/solution.py
@@ -11,7 +11,6 @@
 
 XM = 128
 ALIGN = 16
-CHUNKS = 8
 OUT_CHUNKS = 8
 VALUES_LIMIT = 16 * 2**20
 VMEM_LIMIT = 40 * 2**20
@@ -56,7 +55,7 @@
     nf, ncol, near, early, starts_in, fac_in, prep, wts, fwd_in, bwd_in, win_in, fmap, qtab,
     terms, values, maps, starts_out,
     starts, fac, fwd, bwd, win, pv, qv, wv, send1, recv1, acc, grid, send2, ctab, svec, sall, fv, wdup,
-    ld, s1, r1, s2, sd, sx, sp, rt, ss, rs,
+    ld, s1, r1, s2, sd, sx, sp, ro_near, ro_far, rx_near, rx_far, rp, ss, rs,
 ):
     me = lax.axis_index("facet")
     c = lax.axis_index("col")
@@ -68,55 +67,63 @@
     xa, width = wts.shape[1:]
     half = width // 2
     oc = fmap.shape[0]
-    chunks = CHUNKS
     deep = nf <= 8
-    step = blocks // chunks
+
+    bits = [1 << b for b in range((nf - 1).bit_length())] if pow2 else []
+    flips = [b - 2 * b * lax.rem(lax.div(me, b), 2) for b in bits]
+    across = [lax.rem(xq + q, nx) * 2 + core for q in range(nx)]
+    behind = [lax.rem(xq + nx - q, nx) * 2 + core for q in range(nx)]
 
     def peer(i):
         if not pow2:
             return lax.rem(me + i, nf)
-        out, b = 0, 1
-        while b < nf:
-            mb, ib = lax.rem(lax.div(me, b), 2), lax.rem(lax.div(i, b), 2)
-            out = out + b * (mb + ib - 2 * mb * ib)
-            b *= 2
+        out = me
+        for b, flip in zip(bits, flips):
+            if isinstance(i, int):
+                out = out + flip if i & b else out
+            else:
+                out = out + flip * lax.rem(lax.div(i, b), 2)
         return out
 
     def source(i):
         return peer(i) if pow2 else lax.rem(me + nf - i, nf)
 
-    def across(q):
-        return lax.rem(xq + q, nx) * 2 + core
+    def each(first, last, step):
+        if not deep:
+            pl.loop(first, last)(step)
+            return
+        for i in range(first, last):
+            step(i)
+
+    def each_down(first, last, step):
+        each(0, last - first, lambda k: step(last - 1 - k))
 
     barrier = pltpu.get_barrier_semaphore()
 
-    @pl.loop(1, nf)
-    def _(i):
+    def greet(i):
         pl.semaphore_signal(barrier, inc=1, device_id={"facet": peer(i)}, device_id_type=MESH)
+
+    each(1, nf, greet)
 
     for i in range(1, ncol):
         pl.semaphore_signal(
             barrier, inc=1, device_id={"col": lax.rem(c + i, ncol)}, device_id_type=MESH
         )
 
-    @pl.loop(1, near)
-    def _(i):
+    def greet_across(i):
         for q in range(1, nx):
             pl.semaphore_signal(
-                barrier, inc=1, device_id={"facet": peer(i), "col": across(q)}, device_id_type=MESH
+                barrier, inc=1, device_id={"facet": peer(i), "col": across[q]}, device_id_type=MESH
             )
 
-    loads = [
-        pltpu.make_async_copy(
-            prep.at[:, pl.ds(k * step, step)], pv.at[:, pl.ds(k * step, step)], ld.at[k]
-        )
-        for k in range(chunks)
-    ]
+    each(1, near, greet_across)
+
+    strip_load = pltpu.make_async_copy(prep, pv, ld.at[0])
     small = [(starts_in, starts), (fac_in, fac), (fwd_in, fwd)]
     later = [(win_in, win), (fmap, fv), (bwd_in, bwd), (wts, wv), (qtab, qv)]
-    small = [pltpu.make_async_copy(*pair, ld.at[chunks + k]) for k, pair in enumerate(small)]
-    later = [pltpu.make_async_copy(*pair, ld.at[chunks + 3 + k]) for k, pair in enumerate(later)]
-    for copy in small + loads + later:
+    small = [pltpu.make_async_copy(*pair, ld.at[1 + k]) for k, pair in enumerate(small)]
+    later = [pltpu.make_async_copy(*pair, ld.at[4 + k]) for k, pair in enumerate(later)]
+    for copy in [*small, strip_load, *later]:
         copy.start()
     win_load, f_load, b_load, w_load, q_load = later
     for copy in small:
@@ -132,31 +139,42 @@
             device_id=where, device_id_type=MESH,
         )
 
-    def send_first(h, j):
-        return remote(send1.at[h, j], recv1.at[h, me], s1.at[h, j], r1.at[h, me], facet=j)
-
-    def recv_first(h, j):
-        return remote(send1.at[h, j], recv1.at[h, j], s1.at[h, j], r1.at[h, j], facet=j)
-
-    def send_second(h, j):
-        return remote(send2.at[h, j], terms.at[c, me, h], s2.at[h, j], rt.at[c, me, h], facet=j)
-
-    def send_direct(h, j, q):
+    def send_first(h, i, far):
+        j = peer(i)
+        return remote(send1.at[h, j], recv1.at[h, me], s1.at[h], r1.at[h, far], facet=j)
+
+    def own_arrival(h, i, far):
+        return ro_far.at[h, i - near] if far else ro_near.at[h]
+
+    def across_arrival(h, i, q, far):
+        return rx_far.at[q - 1, h, i - near] if far else rx_near.at[q - 1, h]
+
+    def send_second(h, i, far):
+        j = peer(i)
+        arrived = own_arrival(h, i, far)
+        return remote(send2.at[h, j], terms.at[c, me, h], s2.at[h], arrived, facet=j)
+
+    def send_direct(h, i, q):
+        j = peer(i)
         return remote(
-            send2.at[h, j], terms.at[c, me, h], sd.at[q, j, h], rt.at[c, me, h],
-            facet=j, col=across(q),
+            send2.at[h, j], terms.at[c, me, h], sd.at[q - 1, h], across_arrival(h, i, q, 0),
+            facet=j, col=across[q],
         )
 
-    def arrival(cc, j, h):
-        return remote(send2.at[h, j], terms.at[cc, j, h], s2.at[h, j], rt.at[cc, j, h], facet=j)
-
-    def forward_x(src, j, h, q):
-        return remote(
-            src, terms.at[c, j, h], sx.at[q, j, h], rt.at[c, j, h], col=across(q)
-        )
-
-    def forward_partner(src, cc, j, h):
-        return remote(src, terms.at[cc, j, h], sp.at[cc, j, h], rt.at[cc, j, h], col=partner)
+    def forward_x(h, i, q, far):
+        block = terms.at[c, source(i), h]
+        arrived = across_arrival(h, i, q, far)
+        return remote(block, block, sx.at[q - 1, h], arrived, col=across[q])
+
+    def forward_partner(cc, h, i, far):
+        block = terms.at[cc, source(i), h]
+        return remote(block, block, sp.at[h], rp.at[far * (1 + h)], col=partner)
+
+    def sent(block, sem):
+        remote(block, block, sem, rs.at[0], col=partner).wait_send()
+
+    def received(block, sem):
+        remote(block, block, ss.at[0], sem, col=partner).wait_recv()
 
     row_d = iota((XM, 2 * XM), 1) - iota((XM, 2 * XM), 0)
     fwd_table = fwd[...]
@@ -164,8 +182,8 @@
     def contribution(j, dst):
         start = starts[j]
         block = lax.div(start, XM)
-        shift = lax.rem(start, XM)
-        above = lax.rem(block + 1, blocks)
+        shift = start - block * XM
+        above = jnp.where(block + 1 == blocks, 0, block + 1)
         top = jnp.concatenate([pv[0, block], pv[1, block]], axis=1)
         low = jnp.concatenate([pv[0, above], pv[1, above]], axis=1)
         picked = mm(one_hot(row_d == shift), jnp.concatenate([top, low], axis=0))
@@ -193,27 +211,23 @@
                 [upper[:half], lower[:half], upper[half:], lower[half:]], axis=0
             )
 
-    for copy in loads:
-        copy.wait()
+    strip_load.wait()
     pl.semaphore_wait(barrier, nf - 1 + ncol - 1 + (near - 1) * (nx - 1))
 
-    @pl.loop(1, nf, unroll=deep)
-    def _(i):
-        j = peer(nf - i)
-        contribution(j, send1)
-        send_first(0, j).start()
-
-    @pl.loop(1, nf)
-    def _(i):
-        send_first(1, peer(nf - i)).start()
+    def first(i, far):
+        contribution(peer(i), send1)
+        send_first(0, i, far).start()
+
+    each_down(near, nf, lambda i: first(i, 1))
+    each_down(1, near, lambda i: first(i, 0))
+    each_down(near, nf, lambda i: send_first(1, i, 1).start())
+    each_down(1, near, lambda i: send_first(1, i, 0).start())
 
     contribution(me, recv1)
 
-    start_sends = []
     for i in range(1, ncol):
         to = lax.rem(c + i, ncol)
-        start_sends.append(remote(svec, sall.at[c], ss.at[i], rs.at[c], col=to))
-        start_sends[-1].start()
+        remote(svec, sall.at[c], ss.at[0], rs.at[0], col=to).start()
     sall[c] = svec[...]
     window_maps()
 
@@ -252,15 +266,16 @@
         return prod[:n] + jnp.where(minus, -crossed, crossed)
 
     q_load.wait()
-    own_copies = []
     for h in range(2):
         acc[...] = place(h, me)
 
-        @pl.loop(1, nf)
-        def _(i):
-            j = source(nf - i)
-            recv_first(h, j).wait_recv()
-            acc[...] += place(h, j)
+        def gather(i):
+            acc[...] += place(h, source(i))
+
+        received(recv1.at[h, pl.ds(0, near - 1)], r1.at[h, 0])
+        each(1, near, gather)
+        received(recv1.at[h, pl.ds(0, nf - near)], r1.at[h, 1])
+        each(near, nf, gather)
 
         table = qv[...]
         spectrum = twist(mm(table, acc[...].astype(BF16)), False)
@@ -272,121 +287,75 @@
         def back(j):
             return twist(mm(ctab[j], grid[...]), False).astype(BF16)
 
-        send2[h, me] = back(me)
-        copy = pltpu.make_async_copy(
-            send2.at[h, me], terms.at[c, me, h], ld.at[chunks + 8 + h]
-        )
-        copy.start()
-        own_copies.append(copy)
+        terms[c, me, h] = back(me)
         for q in range(1, nx):
-            forward_x(send2.at[h, me], me, h, q).start()
-        forward_partner(send2.at[h, me], c, me, h).start()
-
-        @pl.loop(1, near, unroll=deep)
-        def _(i):
+            forward_x(h, 0, q, 0).start()
+        forward_partner(c, h, 0, 0).start()
+
+        def second(i, far):
             j = peer(i)
             send2[h, j] = back(j)
-            send_second(h, j).start()
+            send_second(h, i, far).start()
+
+        def second_near(i):
+            second(i, 0)
             for q in range(1, nx):
-                send_direct(h, j, q).start()
-
-        @pl.loop(near, nf, unroll=deep)
-        def _(i):
-            j = peer(i)
-            send2[h, j] = back(j)
-            send_second(h, j).start()
-
-    for copy in own_copies:
-        copy.wait()
-    for i in range(1, ncol):
-        start_sends[i - 1].wait_send()
-        frm = lax.rem(c + ncol - i, ncol)
-        remote(svec, sall.at[frm], ss.at[i], rs.at[frm], col=frm).wait_recv()
-    starts_copy = pltpu.make_async_copy(sall, starts_out, ld.at[chunks + 10])
+                send_direct(h, i, q).start()
+
+        each(1, near, second_near)
+        each(near, nf, lambda i: second(i, 1))
+
+    sent(sall.at[pl.ds(0, ncol - 1)], ss.at[0])
+    received(sall.at[pl.ds(0, ncol - 1)], rs.at[0])
+    starts_copy = pltpu.make_async_copy(sall, starts_out, ld.at[9])
     starts_copy.start()
 
     def relay_near(h):
-        @pl.loop(1, near)
-        def _(i):
-            j = source(i)
-            arrival(c, j, h).wait_recv()
-            forward_partner(terms.at[c, j, h], c, j, h).start()
-
-        @pl.loop(0, near)
-        def _(i):
-            relay_across(source(i), h)
-
-    def relay_far(j, h):
-        arrival(c, j, h).wait_recv()
+        received(terms.at[0, pl.ds(0, near - 1), h], ro_near.at[h])
+        each(1, near, lambda i: forward_partner(c, h, i, 0).start())
         for q in range(1, nx):
-            forward_x(terms.at[c, j, h], j, h, q).start()
-        forward_partner(terms.at[c, j, h], c, j, h).start()
-
-    def relay_across(j, h):
+            received(terms.at[0, pl.ds(0, near), h], rx_near.at[q - 1, h])
+            each(0, near, lambda i: forward_partner(behind[q], h, i, 0).start())
+
+    def relay_far(i, h):
+        received(terms.at[c, source(i), h], own_arrival(h, i, 1))
         for q in range(1, nx):
-            cc = across(q)
-            arrival(cc, j, h).wait_recv()
-            forward_partner(terms.at[cc, j, h], cc, j, h).start()
-
-    def from_partner(j, h):
-        for q in range(nx):
-            arrival(lax.rem(xq + q, nx) * 2 + 1 - core, j, h).wait_recv()
-
-    @pl.loop(near, nf)
-    def _(i):
-        relay_far(source(i), 0)
-
+            forward_x(h, i, q, 1).start()
+        forward_partner(c, h, i, 1).start()
+
+    def relay_across(i, h):
+        for q in range(1, nx):
+            received(terms.at[behind[q], source(i), h], across_arrival(h, i, q, 1))
+            forward_partner(behind[q], h, i, 1).start()
+
+    def relay_both(i):
+        relay_far(i, 1)
+        relay_across(i, 0)
+
+    def map_near(i):
+        j = source(i)
+        for k in range(ncol):
+            values[k, i] = mm(jnp.concatenate([terms[k, j, 0], terms[k, j, 1]], axis=1), maps[k])
+
+    each(near, nf, lambda i: relay_far(i, 0))
     relay_near(0)
     relay_near(1)
-
-    @pl.loop(near, nf)
-    def _(i):
-        relay_far(source(i), 1)
-        relay_across(source(i), 0)
-
-    @pl.loop(0, near)
-    def _(i):
-        j = source(i)
-        from_partner(j, 0)
-        from_partner(j, 1)
-        if early:
-            for k in range(ncol):
-                values[k, i] = mm(jnp.concatenate([terms[k, j, 0], terms[k, j, 1]], axis=1), maps[k])
-
-    @pl.loop(near, nf)
-    def _(i):
-        relay_across(source(i), 1)
-
-    @pl.loop(near, nf)
-    def _(i):
-        from_partner(source(i), 0)
-        from_partner(source(i), 1)
+    each(near, nf, relay_both)
+    received(terms.at[pl.ds(0, nx), pl.ds(0, near)], rp.at[0])
+    if early:
+        each(0, near, map_near)
+    each(near, nf, lambda i: relay_across(i, 1))
+    for h in range(2):
+        received(terms.at[pl.ds(0, nx), pl.ds(0, nf - near), h], rp.at[1 + h])
 
     starts_copy.wait()
     for h in range(2):
-        @pl.loop(0, nf)
-        def _(j):
-            for q in range(nx):
-                forward_partner(terms.at[c, j, h], across(q), j, h).wait_send()
-
+        sent(send1.at[h, pl.ds(0, nf - 1)], s1.at[h])
+        sent(send2.at[h, pl.ds(0, nf - 1)], s2.at[h])
+        sent(terms.at[pl.ds(0, nx), :, h], sp.at[h])
         for q in range(1, nx):
-            forward_x(send2.at[h, me], me, h, q).wait_send()
-
-        @pl.loop(near, nf)
-        def _(i):
-            j = source(i)
-            for q in range(1, nx):
-                forward_x(terms.at[c, j, h], j, h, q).wait_send()
-
-        @pl.loop(1, near)
-        def _(i):
-            for q in range(1, nx):
-                send_direct(h, peer(i), q).wait_send()
-
-        @pl.loop(1, nf)
-        def _(i):
-            send_first(h, peer(i)).wait_send()
-            send_second(h, peer(i)).wait_send()
+            sent(terms.at[0, pl.ds(0, near - 1), h], sd.at[q - 1, h])
+            sent(terms.at[0, pl.ds(0, nf - near + 1), h], sx.at[q - 1, h])
 
 
 def image_gain(nf, xa):
@@ -439,17 +408,13 @@
     gather(split, nf, mapped)
 
     chunk = own_rows // OUT_CHUNKS
-    copies = []
     for k in range(OUT_CHUNKS):
         rows = pl.ds(k * chunk, chunk)
         src = pl.ds(XM + k * chunk, chunk)
         stage[0, rows, :] = acc[src, :oc].astype(BF16)
         stage[1, rows, :] = acc[src, oc:].astype(BF16)
-        copy = pltpu.make_async_copy(stage.at[:, rows, :], out.at[:, rows, :], osem.at[k])
-        copy.start()
-        copies.append(copy)
-    for copy in copies:
-        copy.wait()
+        pltpu.make_async_copy(stage.at[:, rows, :], out.at[:, rows, :], osem.at[0]).start()
+    pltpu.make_async_copy(stage, out, osem.at[0]).wait()
 
 
 def body(prepared, sub_off, fac_off, win_col, vis_weights):
@@ -465,6 +430,7 @@
     starts = sub_off[:, 0]
     lanes = -(-nf // 128) * 128
     near = nf // 2 if nf & (nf - 1) == 0 else 1
+    nx = ncol // 2
     early = ncol * near * XM * 2 * oc * 4 <= VALUES_LIMIT
 
     forward, backward = window_tables(XM)
@@ -510,9 +476,10 @@
             pltpu.VMEM((ncol, 8, lanes), jnp.int32),
             pltpu.VMEM(out_map.shape, BF16),
             pltpu.VMEM((2, 2, xa, width), F32),
-            dma((CHUNKS + 11,)), dma((2, nf)), dma((2, nf)), dma((2, nf)),
-            dma((ncol, nf, 2)), dma((ncol, nf, 2)), dma((ncol, nf, 2)), dma((ncol, nf, 2)),
-            dma((ncol,)), dma((ncol,)),
+            dma((10,)), dma((2,)), dma((2, 2)), dma((2,)),
+            dma((nx - 1, 2)), dma((nx - 1, 2)), dma((2,)),
+            dma((2,)), dma((2, nf - near)), dma((nx - 1, 2)), dma((nx - 1, 2, nf - near)), dma((3,)),
+            dma((1,)), dma((1,)),
         ],
         compiler_params=pltpu.CompilerParams(
             collective_id=0, has_side_effects=True, vmem_limit_bytes=VMEM_LIMIT
@@ -529,7 +496,7 @@
         scratch_shapes=[
             pltpu.VMEM((own_rows + 2 * XM + ALIGN, 2 * oc), F32),
             pltpu.VMEM((2, own_rows, oc), BF16),
-            dma((OUT_CHUNKS,)),
+            dma((1,)),
         ],
         compiler_params=pltpu.CompilerParams(vmem_limit_bytes=VMEM_LIMIT),
         name="finish",

time: 43.8 us -> 40.4 us (0.922)
  Pallas kernels: 43.8 us -> 40.4 us
    pallas_call x1, Pallas kernels: 39.7 us -> 36.7 us  [body(): pl.pallas_call(functools.partial(exchange_kernel, nf, ncol, near, early),...]
where the time goes in v2:
time: 40.4 us
  Pallas kernels  40.4 us (100%)
    pallas_call x1, Pallas kernels, body(): pl.pallas_call(functools.partial(exchange_kernel, nf, ncol, near, early),...  36.7 us
    pallas_call x1, Pallas kernels, body(): pl.pallas_call(functools.partial(finish_kernel, nf, ncol, near, early), o...  3.73 us

profile of v2, /device:TPU:0, one launch (start us, length us, event | category | flops | bytes accessed | tf_op | source)
XLA Modules:
  0.0 40.4 jit_solution(10593887124364135846)
XLA Ops:
  0.0 36.7 %exchange.1 = (bf16[4,8,2,128,128]{4,3,2,1,0:T(8,128)(2,1)S(1)}, f32[4,4,128,512]{3,2,1,0:T(8,128)S(1)}, bf16[4,256,512]{2,1,0:T(8,128)(2,1)S(1)}, s32[4,8,128]{2,1,0:T(8,128)S(4)}) custom-call(s32[8]{0:T(128)} %bitcast.6, s32[8]{0:T(128)} %fac_in.1, bf16[2,64,128,128]{3,2,1,0:T(8,128)(2,1)} %bitcast.4, bf16[2,512,128]{2,1,0:T(8,128)(2,1)} %bitcast.5, ...), custom_call_target="tpu_custom_call" | custom-call | tf_op jit(solution)/shard_map/exchange/pallas_call | solution.py:450
  36.7 3.7 %finish.1 = bf16[2,2048,256]{2,1,0:T(8,128)(2,1)} custom-call(s32[4,8,128]{2,1,0:T(8,128)S(4)} %get-tuple-element.9.starts_all, bf16[4,8,2,128,128]{4,3,2,1,0:T(8,128)(2,1)S(1)} %get-tuple-element.10.terms, f32[4,4,128,512]{3,2,1,0:T(8,128)S(1)} %get-tuple-element.11.values, bf16[4,256,512]{2,1,0:T(8,128)(2,1)S(1)} %get-tuple-element.12.maps), custom_call_target="tpu_custom_call" | custom-call | tf_op jit(solution)/shard_map/finish/pallas_call | solution.py:491

commit v3 on v2

--- a/solution.py
+++ b/solution.py
@@ -12,7 +12,7 @@
 XM = 128
 ALIGN = 16
 OUT_CHUNKS = 8
-VALUES_LIMIT = 16 * 2**20
+TABLE_LIMIT = 16 * 2**20
 VMEM_LIMIT = 40 * 2**20
 MESH = pl.DeviceIdType.MESH
 F32 = jnp.float32
@@ -52,9 +52,9 @@
 
 
 def exchange_kernel(
-    nf, ncol, near, early, starts_in, fac_in, prep, wts, fwd_in, bwd_in, win_in, fmap, qtab,
+    nf, ncol, near, early, folded, starts_in, fac_in, prep, wts, fwd_in, bwd_in, win_in, fmap, qtab,
     terms, values, maps, starts_out,
-    starts, fac, fwd, bwd, win, pv, qv, wv, send1, recv1, acc, grid, send2, ctab, svec, sall, fv, wdup,
+    starts, fac, fwd, bwd, win, pv, qv, wv, send1, recv1, acc, send2, places, shifts, ctab, svec, sall, fv, wdup,
     ld, s1, r1, s2, sd, sx, sp, ro_near, ro_far, rx_near, rx_far, rp, ss, rs,
 ):
     me = lax.axis_index("facet")
@@ -141,7 +141,7 @@
 
     def send_first(h, i, far):
         j = peer(i)
-        return remote(send1.at[h, j], recv1.at[h, me], s1.at[h], r1.at[h, far], facet=j)
+        return remote(send1.at[h, j], recv1.at[h, i], s1.at[h], r1.at[h, far], facet=j)
 
     def own_arrival(h, i, far):
         return ro_far.at[h, i - near] if far else ro_near.at[h]
@@ -179,7 +179,7 @@
     row_d = iota((XM, 2 * XM), 1) - iota((XM, 2 * XM), 0)
     fwd_table = fwd[...]
 
-    def contribution(j, dst):
+    def contribution(j, dst, at):
         start = starts[j]
         block = lax.div(start, XM)
         shift = start - block * XM
@@ -191,8 +191,8 @@
         re = prod[:XM, :width] - prod[XM:, width:]
         im = prod[:XM, width:] + prod[XM:, :width]
         first = iota(re.shape, 1) < half
-        dst[0, j] = jnp.where(first, re, pltpu.roll(im, half, 1)).astype(BF16)
-        dst[1, j] = jnp.where(first, pltpu.roll(re, half, 1), im).astype(BF16)
+        dst[0, at] = jnp.where(first, re, pltpu.roll(im, half, 1)).astype(BF16)
+        dst[1, at] = jnp.where(first, pltpu.roll(re, half, 1), im).astype(BF16)
 
     def window_maps():
         win_load.wait()
@@ -215,7 +215,7 @@
     pl.semaphore_wait(barrier, nf - 1 + ncol - 1 + (near - 1) * (nx - 1))
 
     def first(i, far):
-        contribution(peer(i), send1)
+        contribution(peer(i), send1, peer(i))
         send_first(0, i, far).start()
 
     each_down(near, nf, lambda i: first(i, 1))
@@ -223,26 +223,22 @@
     each_down(near, nf, lambda i: send_first(1, i, 1).start())
     each_down(1, near, lambda i: send_first(1, i, 0).start())
 
-    contribution(me, recv1)
+    contribution(me, recv1, 0)
 
     for i in range(1, ncol):
         to = lax.rem(c + i, ncol)
         remote(svec, sall.at[c], ss.at[0], rs.at[0], col=to).start()
     sall[c] = svec[...]
-    window_maps()
-
-    b_load.wait()
-    turn_d = iota((XM, XM), 0) - iota((XM, XM), 1)
-    turn_by = lax.rem(starts[me], ALIGN)
-    turn = (turn_d == turn_by) | (turn_d == turn_by - XM)
-    turned = mm(one_hot(turn), bwd[...]).astype(BF16)
-    turned = jnp.concatenate([turned[:, :XM], turned[:, XM:]], axis=0)
+
+    grid_d = iota((xa, XM), 0) - iota((xa, XM), 1)
     back_d = iota((XM, xa), 1) - iota((XM, xa), 0)
 
-    @pl.loop(0, nf, unroll=deep)
-    def _(j):
-        hit = (back_d == fac[j]) | (back_d == fac[j] - xa)
-        ctab[j] = mm(turned, one_hot(hit)).astype(BF16)
+    def hit(diff, j):
+        return one_hot((diff == fac[j]) | (diff == fac[j] - xa))
+
+    if folded:
+        for i in range(nf):
+            places[:, i * XM : (i + 1) * XM] = hit(grid_d, source(i))
 
     w_load.wait()
     near_lane = iota((xa, width), 1) < half
@@ -252,40 +248,68 @@
         wdup[0, p] = jnp.where(near_lane, w, swapped)
         wdup[1, p] = jnp.where(near_lane, swapped, w)
 
-    grid_d = iota((xa, XM), 0) - iota((xa, XM), 1)
-
-    def place(h, j):
-        hit = (grid_d == fac[j]) | (grid_d == fac[j] - xa)
-        return mm(one_hot(hit), recv1[h, j])
-
-    def twist(prod, conj):
+    b_load.wait()
+    turn_d = iota((XM, XM), 0) - iota((XM, XM), 1)
+    turn_by = lax.rem(starts[me], ALIGN)
+    turn = (turn_d == turn_by) | (turn_d == turn_by - XM)
+    turned = mm(one_hot(turn), bwd[...]).astype(BF16)
+    turned = jnp.concatenate([turned[:, :XM], turned[:, XM:]], axis=0)
+
+    q_load.wait()
+    column = iota((nf, xa), 0)
+    at_row = jnp.zeros((nf, xa), jnp.int32)
+    at_row = lax.fori_loop(0, nf, lambda j, v: jnp.where(column == j, fac[j], v), at_row)
+    picks = one_hot(iota((nf, xa), 1) == at_row)
+    unit = math.sqrt(nf * XM) * image_gain(nf, xa)
+    shifts[0] = mm(picks, qv[:xa]) * unit
+    shifts[1] = mm(picks, qv[xa:]) * -unit
+    with_re = mm(turned, qv[:XM])
+    with_im = mm(turned, qv[xa : xa + XM])
+    base_re = with_re[:XM] + with_im[XM:]
+    base_im = with_re[XM:] - with_im[:XM]
+
+    def back_table(j):
+        re, im = shifts[0, pl.ds(j, 1), :], shifts[1, pl.ds(j, 1), :]
+        ctab[j, :XM] = (base_re * re - base_im * im).astype(BF16)
+        ctab[j, XM:] = (base_re * im + base_im * re).astype(BF16)
+
+    each(0, nf, back_table)
+
+    def twist(prod):
         n = prod.shape[0] // 2
         crossed = pltpu.roll(prod[n:], half, 1)
         first = iota(crossed.shape, 1) < half
-        minus = jnp.logical_not(first) if conj else first
-        return prod[:n] + jnp.where(minus, -crossed, crossed)
-
-    q_load.wait()
+        return prod[:n] + jnp.where(first, -crossed, crossed)
+
+    def arrived(h, first, last):
+        return recv1[h, first:last].reshape((last - first) * XM, width)
+
     for h in range(2):
-        acc[...] = place(h, me)
-
-        def gather(i):
-            acc[...] += place(h, source(i))
-
-        received(recv1.at[h, pl.ds(0, near - 1)], r1.at[h, 0])
-        each(1, near, gather)
-        received(recv1.at[h, pl.ds(0, nf - near)], r1.at[h, 1])
-        each(near, nf, gather)
-
-        table = qv[...]
-        spectrum = twist(mm(table, acc[...].astype(BF16)), False)
+        near_blocks, far_blocks = recv1.at[h, pl.ds(0, near - 1)], recv1.at[h, pl.ds(0, nf - near)]
+        if folded:
+            split = near * XM
+            received(near_blocks, r1.at[h, 0])
+            acc[...] = mm(places[:, :split], arrived(h, 0, near))
+            received(far_blocks, r1.at[h, 1])
+            acc[...] += mm(places[:, split:], arrived(h, near, nf))
+        else:
+            acc[...] = mm(hit(grid_d, me), recv1[h, 0])
+
+            def gather(i):
+                acc[...] += mm(hit(grid_d, source(i)), recv1[h, i])
+
+            received(near_blocks, r1.at[h, 0])
+            each(1, near, gather)
+            received(far_blocks, r1.at[h, 1])
+            each(near, nf, gather)
+        prod = mm(qv[...], acc[...].astype(BF16))
+        spectrum = twist(prod)
         crossed = wdup[h, 1] * pltpu.roll(spectrum, half, 1)
         weighted = wdup[h, 0] * spectrum + jnp.where(near_lane, -crossed, crossed)
-        image = twist(mm(table, weighted.astype(BF16)), True)
-        grid[...] = (image * image_gain(nf, xa)).astype(BF16)
+        weighted = weighted.astype(BF16)
 
         def back(j):
-            return twist(mm(ctab[j], grid[...]), False).astype(BF16)
+            return twist(mm(ctab[j], weighted)).astype(BF16)
 
         terms[c, me, h] = back(me)
         for q in range(1, nx):
@@ -304,6 +328,8 @@
 
         each(1, near, second_near)
         each(near, nf, lambda i: second(i, 1))
+        if h == 0:
+            window_maps()
 
     sent(sall.at[pl.ds(0, ncol - 1)], ss.at[0])
     received(sall.at[pl.ds(0, ncol - 1)], rs.at[0])
@@ -313,6 +339,8 @@
     def relay_near(h):
         received(terms.at[0, pl.ds(0, near - 1), h], ro_near.at[h])
         each(1, near, lambda i: forward_partner(c, h, i, 0).start())
+
+    def relay_across_near(h):
         for q in range(1, nx):
             received(terms.at[0, pl.ds(0, near), h], rx_near.at[q - 1, h])
             each(0, near, lambda i: forward_partner(behind[q], h, i, 0).start())
@@ -339,8 +367,10 @@
 
     each(near, nf, lambda i: relay_far(i, 0))
     relay_near(0)
+    relay_across_near(0)
+    each(near, nf, relay_both)
     relay_near(1)
-    each(near, nf, relay_both)
+    relay_across_near(1)
     received(terms.at[pl.ds(0, nx), pl.ds(0, near)], rp.at[0])
     if early:
         each(0, near, map_near)
@@ -431,7 +461,8 @@
     lanes = -(-nf // 128) * 128
     near = nf // 2 if nf & (nf - 1) == 0 else 1
     nx = ncol // 2
-    early = ncol * near * XM * 2 * oc * 4 <= VALUES_LIMIT
+    early = ncol * near * XM * 2 * oc * 4 <= TABLE_LIMIT
+    folded = xa * nf * XM * 2 <= TABLE_LIMIT // 4
 
     forward, backward = window_tables(XM)
     q_table = stacked(*dft(xa, -1.0, 1.0 / math.sqrt(nf * XM)), 0)
@@ -448,7 +479,7 @@
     )
     held = (ncol, near, XM, 2 * oc) if early else (8, 128)
     results = pl.pallas_call(
-        functools.partial(exchange_kernel, nf, ncol, near, early),
+        functools.partial(exchange_kernel, nf, ncol, near, early, folded),
         out_shape=(
             pltpu.VMEM((ncol, nf, 2, XM, width), BF16),
             pltpu.VMEM(held, F32),
@@ -469,8 +500,9 @@
             halves,
             halves,
             pltpu.VMEM((xa, width), F32),
-            pltpu.VMEM((xa, width), BF16),
             halves,
+            pltpu.VMEM((xa, nf * XM) if folded else (8, 128), BF16),
+            pltpu.VMEM((2, nf, xa), F32),
             pltpu.VMEM((nf, 2 * XM, xa), BF16),
             pltpu.VMEM((8, lanes), jnp.int32),
             pltpu.VMEM((ncol, 8, lanes), jnp.int32),

time: 40.4 us -> 39.9 us (0.988)
  Pallas kernels: 40.4 us -> 39.7 us
    pallas_call x1, Pallas kernels: 36.7 us -> 35.9 us  [body(): pl.pallas_call(functools.partial(exchange_kernel, nf, ncol, near, early,...]
where the time goes in v3:
time: 39.9 us; the launch traced here: 39.7 us
  Pallas kernels  39.7 us (99%)
    pallas_call x1, Pallas kernels, body(): pl.pallas_call(functools.partial(exchange_kernel, nf, ncol, near, early,...  35.9 us
    pallas_call x1, Pallas kernels, body(): pl.pallas_call(functools.partial(finish_kernel, nf, ncol, near, early), o...  3.88 us

profile of v3, /device:TPU:0, one launch (start us, length us, event | category | flops | bytes accessed | tf_op | source)
XLA Modules:
  0.0 39.7 jit_solution(15261073849843686491)
XLA Ops:
  0.0 35.9 %exchange.1 = (bf16[4,8,2,128,128]{4,3,2,1,0:T(8,128)(2,1)S(1)}, f32[4,4,128,512]{3,2,1,0:T(8,128)S(1)}, bf16[4,256,512]{2,1,0:T(8,128)(2,1)S(1)}, s32[4,8,128]{2,1,0:T(8,128)S(4)}) custom-call(s32[8]{0:T(128)} %bitcast.6, s32[8]{0:T(128)} %fac_in.1, bf16[2,64,128,128]{3,2,1,0:T(8,128)(2,1)} %bitcast.4, bf16[2,512,128]{2,1,0:T(8,128)(2,1)} %bitcast.5, ...), custom_call_target="tpu_custom_call" | custom-call | tf_op jit(solution)/shard_map/exchange/pallas_call | solution.py:481
  35.9 3.9 %finish.1 = bf16[2,2048,256]{2,1,0:T(8,128)(2,1)} custom-call(s32[4,8,128]{2,1,0:T(8,128)S(4)} %get-tuple-element.9.starts_all, bf16[4,8,2,128,128]{4,3,2,1,0:T(8,128)(2,1)S(1)} %get-tuple-element.10.terms, f32[4,4,128,512]{3,2,1,0:T(8,128)S(1)} %get-tuple-element.11.values, bf16[4,256,512]{2,1,0:T(8,128)(2,1)S(1)} %get-tuple-element.12.maps), custom_call_target="tpu_custom_call" | custom-call | tf_op jit(solution)/shard_map/finish/pallas_call | solution.py:523

commit v4 on v3

--- a/solution.py
+++ b/solution.py
@@ -220,8 +220,6 @@
 
     each_down(near, nf, lambda i: first(i, 1))
     each_down(1, near, lambda i: first(i, 0))
-    each_down(near, nf, lambda i: send_first(1, i, 1).start())
-    each_down(1, near, lambda i: send_first(1, i, 0).start())
 
     contribution(me, recv1, 0)
 
@@ -275,6 +273,10 @@
 
     each(0, nf, back_table)
 
+    sent(send1.at[0, pl.ds(0, nf - 1)], s1.at[0])
+    each_down(near, nf, lambda i: send_first(1, i, 1).start())
+    each_down(1, near, lambda i: send_first(1, i, 0).start())
+
     def twist(prod):
         n = prod.shape[0] // 2
         crossed = pltpu.roll(prod[n:], half, 1)
@@ -367,20 +369,24 @@
 
     each(near, nf, lambda i: relay_far(i, 0))
     relay_near(0)
+    relay_near(1)
     relay_across_near(0)
-    each(near, nf, relay_both)
-    relay_near(1)
     relay_across_near(1)
     received(terms.at[pl.ds(0, nx), pl.ds(0, near)], rp.at[0])
-    if early:
-        each(0, near, map_near)
+    def relay_map(i):
+        relay_both(i)
+        if early:
+            map_near(i - near)
+
+    each(near, nf, relay_map)
     each(near, nf, lambda i: relay_across(i, 1))
     for h in range(2):
         received(terms.at[pl.ds(0, nx), pl.ds(0, nf - near), h], rp.at[1 + h])
 
     starts_copy.wait()
     for h in range(2):
-        sent(send1.at[h, pl.ds(0, nf - 1)], s1.at[h])
+        if h:
+            sent(send1.at[h, pl.ds(0, nf - 1)], s1.at[h])
         sent(send2.at[h, pl.ds(0, nf - 1)], s2.at[h])
         sent(terms.at[pl.ds(0, nx), :, h], sp.at[h])
         for q in range(1, nx):

time: 39.9 us -> 39.3 us (0.985)
  Pallas kernels: 39.7 us -> 39.1 us
    pallas_call x1, Pallas kernels: 35.9 us -> 35.3 us  [body(): pl.pallas_call(functools.partial(exchange_kernel, nf, ncol, near, early,...]
where the time goes in v4:
time: 39.3 us; the launch traced here: 39.1 us
  Pallas kernels  39.1 us (99%)
    pallas_call x1, Pallas kernels, body(): pl.pallas_call(functools.partial(exchange_kernel, nf, ncol, near, early,...  35.3 us
    pallas_call x1, Pallas kernels, body(): pl.pallas_call(functools.partial(finish_kernel, nf, ncol, near, early), o...  3.73 us

profile of v4, /device:TPU:0, one launch (start us, length us, event | category | flops | bytes accessed | tf_op | source)
XLA Modules:
  0.0 39.1 jit_solution(14074075281465245965)
XLA Ops:
  0.0 35.3 %exchange.1 = (bf16[4,8,2,128,128]{4,3,2,1,0:T(8,128)(2,1)S(1)}, f32[4,4,128,512]{3,2,1,0:T(8,128)S(1)}, bf16[4,256,512]{2,1,0:T(8,128)(2,1)S(1)}, s32[4,8,128]{2,1,0:T(8,128)S(4)}) custom-call(s32[8]{0:T(128)} %bitcast.6, s32[8]{0:T(128)} %fac_in.1, bf16[2,64,128,128]{3,2,1,0:T(8,128)(2,1)} %bitcast.4, bf16[2,512,128]{2,1,0:T(8,128)(2,1)} %bitcast.5, ...), custom_call_target="tpu_custom_call" | custom-call | tf_op jit(solution)/shard_map/exchange/pallas_call | solution.py:487
  35.3 3.7 %finish.1 = bf16[2,2048,256]{2,1,0:T(8,128)(2,1)} custom-call(s32[4,8,128]{2,1,0:T(8,128)S(4)} %get-tuple-element.9.starts_all, bf16[4,8,2,128,128]{4,3,2,1,0:T(8,128)(2,1)S(1)} %get-tuple-element.10.terms, f32[4,4,128,512]{3,2,1,0:T(8,128)S(1)} %get-tuple-element.11.values, bf16[4,256,512]{2,1,0:T(8,128)(2,1)S(1)} %get-tuple-element.12.maps), custom_call_target="tpu_custom_call" | custom-call | tf_op jit(solution)/shard_map/finish/pallas_call | solution.py:529

commit v5 on v4

--- a/solution.py
+++ b/solution.py
@@ -398,7 +398,7 @@
     return math.sqrt(nf * XM) / math.sqrt(xa)
 
 
-def finish_kernel(nf, ncol, near, early, starts_all, terms, values, maps, out, acc, stage, osem):
+def finish_kernel(nf, ncol, near, early, starts_all, terms, values, maps, out, acc, stage, seen, code, osem):
     me = lax.axis_index("facet")
     c = lax.axis_index("col")
     own_rows = out.shape[1]
@@ -416,40 +416,65 @@
     slot = iota((XM, 2 * oc), 0)
     edge = iota((ALIGN, 2 * oc), 0)
 
-    def gather(first, last, value_of):
-        @pl.loop(first * ncol, last * ncol)
+    split = near if early else 0
+    mid = XM + own_rows // 2
+
+    def listed(kind, first, last):
+        def note(cc, i, counts):
+            upper, lower = counts
+            j = source(i)
+            rel = starts_all[cc, 0, j] - base
+            rel = jnp.where(rel < 0, rel + total, rel)
+            rel = jnp.where(rel >= total - XM, rel - total, rel) + XM
+            inside = rel < own_rows + XM
+            is_lower = rel >= mid
+            spot = jnp.where(is_lower, lower, upper)
+            place = jnp.where(is_lower, 1, 0)
+            seen[kind, place, spot] = rel
+            code[kind, place, spot] = i * ncol + cc
+            one = jnp.where(inside, 1, 0)
+            return upper + one * (1 - place), lower + one * place
+
+        zero = jnp.int32(0)
+        counts = (zero, zero)
+        for cc in range(ncol):
+            if nf <= 8:
+                for i in range(first, last):
+                    counts = note(cc, i, counts)
+            else:
+                counts = lax.fori_loop(first, last, lambda i, n: note(cc, i, n), counts)
+        return counts
+
+    def gather(kind, place, count, value_of):
+        @pl.loop(0, count)
         def _(t):
-            i, cc = lax.div(t, ncol), lax.rem(t, ncol)
-            j = source(i)
-            rel = starts_all[cc, 0, j] - base + XM
-            rel = jnp.where(rel < 0, rel + total, rel)
-            rel = jnp.where(rel >= total, rel - total, rel)
-
-            @pl.when(rel < own_rows + XM)
-            def _():
-                value = value_of(cc, i, j)
-                turn = lax.rem(rel, ALIGN)
-                low = pl.multiple_of(rel - turn, ALIGN)
-                acc[pl.ds(low, XM), :] += jnp.where(slot >= turn, value, 0.0)
-                acc[pl.ds(pl.multiple_of(low + XM, ALIGN), ALIGN), :] += jnp.where(
-                    edge < turn, value[:ALIGN], 0.0
-                )
+            rel, term = seen[kind, place, t], code[kind, place, t]
+            i = lax.div(term, ncol)
+            cc = term - i * ncol
+            value = value_of(cc, i, source(i))
+            turn = jnp.bitwise_and(rel, ALIGN - 1)
+            low = pl.multiple_of(rel - turn, ALIGN)
+            acc[pl.ds(low, XM), :] += jnp.where(slot >= turn, value, 0.0)
+            acc[pl.ds(pl.multiple_of(low + XM, ALIGN), ALIGN), :] += jnp.where(
+                edge < turn, value[:ALIGN], 0.0
+            )
 
     def mapped(cc, i, j):
         return mm(jnp.concatenate([terms[cc, j, 0], terms[cc, j, 1]], axis=1), maps[cc])
 
-    split = near if early else 0
-    if early:
-        gather(0, split, lambda cc, i, j: values[cc, i])
-    gather(split, nf, mapped)
-
+    early_counts = listed(0, 0, split) if early else None
+    late_counts = listed(1, split, nf)
     chunk = own_rows // OUT_CHUNKS
-    for k in range(OUT_CHUNKS):
-        rows = pl.ds(k * chunk, chunk)
-        src = pl.ds(XM + k * chunk, chunk)
-        stage[0, rows, :] = acc[src, :oc].astype(BF16)
-        stage[1, rows, :] = acc[src, oc:].astype(BF16)
-        pltpu.make_async_copy(stage.at[:, rows, :], out.at[:, rows, :], osem.at[0]).start()
+    for place in range(2):
+        if early:
+            gather(0, place, early_counts[place], lambda cc, i, j: values[cc, i])
+        gather(1, place, late_counts[place], mapped)
+        for k in range(place * OUT_CHUNKS // 2, (place + 1) * OUT_CHUNKS // 2):
+            rows = pl.ds(k * chunk, chunk)
+            src = pl.ds(XM + k * chunk, chunk)
+            stage[0, rows, :] = acc[src, :oc].astype(BF16)
+            stage[1, rows, :] = acc[src, oc:].astype(BF16)
+            pltpu.make_async_copy(stage.at[:, rows, :], out.at[:, rows, :], osem.at[0]).start()
     pltpu.make_async_copy(stage, out, osem.at[0]).wait()
 
 
@@ -534,6 +559,8 @@
         scratch_shapes=[
             pltpu.VMEM((own_rows + 2 * XM + ALIGN, 2 * oc), F32),
             pltpu.VMEM((2, own_rows, oc), BF16),
+            pltpu.SMEM((2, 2, ncol * nf + 1), jnp.int32),
+            pltpu.SMEM((2, 2, ncol * nf + 1), jnp.int32),
             dma((1,)),
         ],
         compiler_params=pltpu.CompilerParams(vmem_limit_bytes=VMEM_LIMIT),

time: 39.3 us -> 38.1 us (0.969)
  Pallas kernels: 39.1 us -> 37.7 us
    pallas_call x1, Pallas kernels: 3.73 us -> 2.38 us  [body(): pl.pallas_call(functools.partial(finish_kernel, nf, ncol, near, early), o...]
where the time goes in v5:
time: 38.1 us; the launch traced here: 37.7 us
  Pallas kernels  37.7 us (99%)
    pallas_call x1, Pallas kernels, body(): pl.pallas_call(functools.partial(exchange_kernel, nf, ncol, near, early,...  35.3 us
    pallas_call x1, Pallas kernels, body(): pl.pallas_call(functools.partial(finish_kernel, nf, ncol, near, early), o...  2.38 us

profile of v5, /device:TPU:0, one launch (start us, length us, event | category | flops | bytes accessed | tf_op | source)
XLA Modules:
  0.0 37.7 jit_solution(16825025516960132422)
XLA Ops:
  0.0 35.3 %exchange.1 = (bf16[4,8,2,128,128]{4,3,2,1,0:T(8,128)(2,1)S(1)}, f32[4,4,128,512]{3,2,1,0:T(8,128)S(1)}, bf16[4,256,512]{2,1,0:T(8,128)(2,1)S(1)}, s32[4,8,128]{2,1,0:T(8,128)S(4)}) custom-call(s32[8]{0:T(128)} %bitcast.6, s32[8]{0:T(128)} %fac_in.1, bf16[2,64,128,128]{3,2,1,0:T(8,128)(2,1)} %bitcast.4, bf16[2,512,128]{2,1,0:T(8,128)(2,1)} %bitcast.5, ...), custom_call_target="tpu_custom_call" | custom-call | tf_op jit(solution)/shard_map/exchange/pallas_call | solution.py:512
  35.3 2.4 %finish.1 = bf16[2,2048,256]{2,1,0:T(8,128)(2,1)} custom-call(s32[4,8,128]{2,1,0:T(8,128)S(4)} %get-tuple-element.9.starts_all, bf16[4,8,2,128,128]{4,3,2,1,0:T(8,128)(2,1)S(1)} %get-tuple-element.10.terms, f32[4,4,128,512]{3,2,1,0:T(8,128)S(1)} %get-tuple-element.11.values, bf16[4,256,512]{2,1,0:T(8,128)(2,1)S(1)} %get-tuple-element.12.maps), custom_call_target="tpu_custom_call" | custom-call | tf_op jit(solution)/shard_map/finish/pallas_call | solution.py:554

commit v6 on v5

--- a/solution.py
+++ b/solution.py
@@ -12,6 +12,7 @@
 XM = 128
 ALIGN = 16
 OUT_CHUNKS = 8
+GROUP = 3
 TABLE_LIMIT = 16 * 2**20
 VMEM_LIMIT = 40 * 2**20
 MESH = pl.DeviceIdType.MESH
@@ -68,6 +69,7 @@
     half = width // 2
     oc = fmap.shape[0]
     deep = nf <= 8
+    middle = (near + nf) // 2
 
     bits = [1 << b for b in range((nf - 1).bit_length())] if pow2 else []
     flips = [b - 2 * b * lax.rem(lax.div(me, b), 2) for b in bits]
@@ -318,10 +320,11 @@
             forward_x(h, 0, q, 0).start()
         forward_partner(c, h, 0, 0).start()
 
-        def second(i, far):
+        def second(i, far, late=False):
             j = peer(i)
             send2[h, j] = back(j)
-            send_second(h, i, far).start()
+            if not (h and late):
+                send_second(h, i, far).start()
 
         def second_near(i):
             second(i, 0)
@@ -329,7 +332,8 @@
                 send_direct(h, i, q).start()
 
         each(1, near, second_near)
-        each(near, nf, lambda i: second(i, 1))
+        each(near, middle, lambda i: second(i, 1))
+        each(middle, nf, lambda i: second(i, 1, True))
         if h == 0:
             window_maps()
 
@@ -367,7 +371,9 @@
         for k in range(ncol):
             values[k, i] = mm(jnp.concatenate([terms[k, j, 0], terms[k, j, 1]], axis=1), maps[k])
 
-    each(near, nf, lambda i: relay_far(i, 0))
+    each(near, near + 1, lambda i: relay_far(i, 0))
+    each(middle, nf, lambda i: send_second(1, i, 1).start())
+    each(near + 1, nf, lambda i: relay_far(i, 0))
     relay_near(0)
     relay_near(1)
     relay_across_near(0)
@@ -443,21 +449,31 @@
                     counts = note(cc, i, counts)
             else:
                 counts = lax.fori_loop(first, last, lambda i, n: note(cc, i, n), counts)
+        for place in range(2):
+            for k in range(GROUP - 1):
+                seen[kind, place, counts[place] + k] = 0
+                code[kind, place, counts[place] + k] = first * ncol
         return counts
 
     def gather(kind, place, count, value_of):
-        @pl.loop(0, count)
-        def _(t):
-            rel, term = seen[kind, place, t], code[kind, place, t]
+        def load(t):
+            term = code[kind, place, t]
             i = lax.div(term, ncol)
-            cc = term - i * ncol
-            value = value_of(cc, i, source(i))
+            return seen[kind, place, t], value_of(term - i * ncol, i, source(i))
+
+        def add(rel, value):
             turn = jnp.bitwise_and(rel, ALIGN - 1)
             low = pl.multiple_of(rel - turn, ALIGN)
             acc[pl.ds(low, XM), :] += jnp.where(slot >= turn, value, 0.0)
             acc[pl.ds(pl.multiple_of(low + XM, ALIGN), ALIGN), :] += jnp.where(
                 edge < turn, value[:ALIGN], 0.0
             )
+
+        @pl.loop(0, lax.div(count + GROUP - 1, GROUP))
+        def _(t):
+            pairs = [load(t * GROUP + k) for k in range(GROUP)]
+            for rel, value in pairs:
+                add(rel, value)
 
     def mapped(cc, i, j):
         return mm(jnp.concatenate([terms[cc, j, 0], terms[cc, j, 1]], axis=1), maps[cc])
@@ -559,8 +575,8 @@
         scratch_shapes=[
             pltpu.VMEM((own_rows + 2 * XM + ALIGN, 2 * oc), F32),
             pltpu.VMEM((2, own_rows, oc), BF16),
-            pltpu.SMEM((2, 2, ncol * nf + 1), jnp.int32),
-            pltpu.SMEM((2, 2, ncol * nf + 1), jnp.int32),
+            pltpu.SMEM((2, 2, ncol * nf + GROUP), jnp.int32),
+            pltpu.SMEM((2, 2, ncol * nf + GROUP), jnp.int32),
             dma((1,)),
         ],
         compiler_params=pltpu.CompilerParams(vmem_limit_bytes=VMEM_LIMIT),

time: 38.1 us -> 37.6 us (0.987)
  no operation moved by 1% of the time
where the time goes in v6:
time: 37.6 us; the launch traced here: 37.5 us
  Pallas kernels  37.5 us (100%)
    pallas_call x1, Pallas kernels, body(): pl.pallas_call(functools.partial(exchange_kernel, nf, ncol, near, early,...  35.1 us
    pallas_call x1, Pallas kernels, body(): pl.pallas_call(functools.partial(finish_kernel, nf, ncol, near, early), o...  2.44 us

profile of v6, /device:TPU:0, one launch (start us, length us, event | category | flops | bytes accessed | tf_op | source)
XLA Modules:
  0.0 37.5 jit_solution(2381926339324135384)
XLA Ops:
  0.0 35.1 %exchange.1 = (bf16[4,8,2,128,128]{4,3,2,1,0:T(8,128)(2,1)S(1)}, f32[4,4,128,512]{3,2,1,0:T(8,128)S(1)}, bf16[4,256,512]{2,1,0:T(8,128)(2,1)S(1)}, s32[4,8,128]{2,1,0:T(8,128)S(4)}) custom-call(s32[8]{0:T(128)} %bitcast.6, s32[8]{0:T(128)} %fac_in.1, bf16[2,64,128,128]{3,2,1,0:T(8,128)(2,1)} %bitcast.4, bf16[2,512,128]{2,1,0:T(8,128)(2,1)} %bitcast.5, ...), custom_call_target="tpu_custom_call" | custom-call | tf_op jit(solution)/shard_map/exchange/pallas_call | solution.py:528
  35.1 2.4 %finish.1 = bf16[2,2048,256]{2,1,0:T(8,128)(2,1)} custom-call(s32[4,8,128]{2,1,0:T(8,128)S(4)} %get-tuple-element.9.starts_all, bf16[4,8,2,128,128]{4,3,2,1,0:T(8,128)(2,1)S(1)} %get-tuple-element.10.terms, f32[4,4,128,512]{3,2,1,0:T(8,128)S(1)} %get-tuple-element.11.values, bf16[4,256,512]{2,1,0:T(8,128)(2,1)S(1)} %get-tuple-element.12.maps), custom_call_target="tpu_custom_call" | custom-call | tf_op jit(solution)/shard_map/finish/pallas_call | solution.py:570

commit v7 on v6

--- a/solution.py
+++ b/solution.py
@@ -12,7 +12,7 @@
 XM = 128
 ALIGN = 16
 OUT_CHUNKS = 8
-GROUP = 3
+GROUP = 4
 TABLE_LIMIT = 16 * 2**20
 VMEM_LIMIT = 40 * 2**20
 MESH = pl.DeviceIdType.MESH

time: 37.6 us -> 37.9 us (level)
  no operation moved by 1% of the time
where the time goes in v7:
time: 37.9 us; the launch traced here: 37.5 us
  Pallas kernels  37.5 us (99%)
    pallas_call x1, Pallas kernels, body(): pl.pallas_call(functools.partial(exchange_kernel, nf, ncol, near, early,...  35.1 us
    pallas_call x1, Pallas kernels, body(): pl.pallas_call(functools.partial(finish_kernel, nf, ncol, near, early), o...  2.43 us

profile of v7, /device:TPU:0, one launch (start us, length us, event | category | flops | bytes accessed | tf_op | source)
XLA Modules:
  0.0 37.5 jit_solution(13395631746716054922)
XLA Ops:
  0.0 35.1 %exchange.1 = (bf16[4,8,2,128,128]{4,3,2,1,0:T(8,128)(2,1)S(1)}, f32[4,4,128,512]{3,2,1,0:T(8,128)S(1)}, bf16[4,256,512]{2,1,0:T(8,128)(2,1)S(1)}, s32[4,8,128]{2,1,0:T(8,128)S(4)}) custom-call(s32[8]{0:T(128)} %bitcast.6, s32[8]{0:T(128)} %fac_in.1, bf16[2,64,128,128]{3,2,1,0:T(8,128)(2,1)} %bitcast.4, bf16[2,512,128]{2,1,0:T(8,128)(2,1)} %bitcast.5, ...), custom_call_target="tpu_custom_call" | custom-call | tf_op jit(solution)/shard_map/exchange/pallas_call | solution.py:528
  35.1 2.4 %finish.1 = bf16[2,2048,256]{2,1,0:T(8,128)(2,1)} custom-call(s32[4,8,128]{2,1,0:T(8,128)S(4)} %get-tuple-element.9.starts_all, bf16[4,8,2,128,128]{4,3,2,1,0:T(8,128)(2,1)S(1)} %get-tuple-element.10.terms, f32[4,4,128,512]{3,2,1,0:T(8,128)S(1)} %get-tuple-element.11.values, bf16[4,256,512]{2,1,0:T(8,128)(2,1)S(1)} %get-tuple-element.12.maps), custom_call_target="tpu_custom_call" | custom-call | tf_op jit(solution)/shard_map/finish/pallas_call | solution.py:570
